TPU v7x, 256 devices: a whole 4x4x8 slice. The times are simulated.
256 devices in a mesh: space: 64 (over y, x, z_hi, core), batch: 4 (over z_lo).
Axes of the slice: x: 4, y: 4, z: 8 (z_hi: 2, z_lo: 4; z = z_hi * 4 + z_lo), core: 2. Of those that a mesh axis runs over, the one named last changes fastest.
Arguments:
- fields: bfloat16 [4, 64, 32, 32, 256], P('batch', 'space'), may hold values from -6 to 6
- cotangent: bfloat16 [4, 64, 32, 32, 256], P('batch', 'space'), may hold values from -6 to 6
- dw_kernel: float32 [9, 256], replicated, may hold values from -2 to 2
- dw_bias: float32 [256], replicated, may hold values from -3 to 3
- ln_gain: float32 [256], replicated, may hold values from 0.1 to 1.9
- ln_shift: float32 [256], replicated, may hold values from -1.8 to 1.8
- w_in: bfloat16 [256, 1024], replicated, may hold values from -0.375 to 0.375
- b_in: float32 [1024], replicated, may hold values from -3 to 3
- w_out: bfloat16 [1024, 256], replicated, may hold values from -0.1875 to 0.1875
- b_out: float32 [256], replicated, may hold values from -3 to 3
- seam_links: int32 [64, 4], replicated, may hold values from 0 to 511, as said below
- corner_links: int32 [64, 4], replicated, may hold values from 0 to 255, as said below
Outputs:
- blocks: bfloat16 [4, 64, 32, 32, 256], P('batch', 'space')
- grad_fields: bfloat16 [4, 64, 32, 32, 256], P('batch', 'space')
- grad_kernel: float32 [9, 256], replicated
- grad_channels: float32 [4, 256], replicated
- grad_w_in: float32 [256, 1024], replicated
- grad_b_in: float32 [1024], replicated
- grad_w_out: float32 [1024, 256], replicated
Inputs may be any that keep to these rules, and one draw needn't show every extreme that they name: seam_links[t, e] = 8 p + 2 f + r: edge e of tile t meets edge f of tile p, reversed if r = 1. The relation is symmetric: seam_links[p, f] = 8 t + 2 e + r. The four edges of a tile meet four different tiles, none of them the tile itself. corner_links[t, k] = 4 p + j: the cell beyond corner k of tile t is corner cell j of tile p, and corner_links[p, j] = 4 t + k.
All inputs are finite; a program needn't handle non-finite values.
Results may differ from a plain program's by a relative error of at most 0.006.
Values may be sent and summed in bfloat16 or wider, within the bound.
No kernel may reach another device: no remote copies, remote signals or barrier semaphores. Data moves between devices by JAX's collectives and lax.ppermute only.
A program may use at most 64 MiB of HBM per device.

v0:
```python
import functools

import jax
import jax.numpy as jnp
from jax import lax
from jax.experimental import pallas as pl
from jax.experimental.pallas import tpu as pltpu
from jax.sharding import PartitionSpec as P


S = 32
C = 256
H = 1024
SLOT = 72
EDGE = 136
CHUNK = 72
BF = jnp.bfloat16
F32 = jnp.float32
GELU_C = 0.7978845608028654
VMEM = functools.partial(pl.BlockSpec, memory_space=pltpu.VMEM)


def staged_call(kernel, ins, outs, scratch, mib, cost=None):
    n_in, n_out = len(ins), len(outs)
    space = {"vmem": pltpu.VMEM, "smem": pltpu.SMEM}
    in_bufs = [space[w](a.shape, a.dtype) for a, w, _ in ins if w != "here"]
    out_bufs = [pltpu.VMEM(o.shape, o.dtype) for o, to_hbm in outs if to_hbm]
    hbm = pl.BlockSpec(memory_space=pltpu.HBM)

    def body(*refs):
        given, results = refs[:n_in], refs[n_in : n_in + n_out]
        rest = list(refs[n_in + n_out :])
        sems = rest.pop(0)
        stages = [rest.pop(0) for _ in in_bufs]
        drains = [rest.pop(0) for _ in out_bufs]
        args, waits, soon, n = [], {}, [], 0
        for i, (ref, (_, where, late)) in enumerate(zip(given, ins)):
            if where == "here":
                args.append(ref)
                continue
            copy = pltpu.make_async_copy(ref, stages[n], sems.at[n])
            copy.start()
            args.append(stages[n])
            n += 1
            if late:
                waits[i] = copy.wait
            else:
                soon.append(copy)
        for copy in soon:
            copy.wait()
        writes = []
        for ref, (_, to_hbm) in zip(results, outs):
            if to_hbm:
                drain = drains.pop(0)
                writes.append(pltpu.make_async_copy(drain, ref, sems.at[n]))
                args.append(drain)
                n += 1
            else:
                args.append(ref)
        kernel(waits, *args, *rest)
        for copy in writes:
            copy.start()
        for copy in writes:
            copy.wait()

    return pl.pallas_call(
        body,
        out_shape=tuple(o for o, _ in outs),
        in_specs=[VMEM() if w == "here" else hbm for _, w, _ in ins],
        out_specs=tuple(hbm if to_hbm else VMEM() for _, to_hbm in outs),
        scratch_shapes=[pltpu.SemaphoreType.DMA((len(in_bufs) + len(out_bufs) + 1,))]
        + in_bufs
        + out_bufs
        + scratch,
        compiler_params=pltpu.CompilerParams(vmem_limit_bytes=mib * 1024 * 1024),
        cost_estimate=cost,
    )(*(a for a, _, _ in ins))


def put_edges(out_ref, strips, cells):
    for e in range(4):
        out_ref[pl.ds(S * e, S), :] = strips[e].astype(BF)
    cells8 = jnp.concatenate([c.reshape(1, C) for c in cells] + [jnp.zeros((4, C), F32)], axis=0)
    out_ref[pl.ds(4 * S, 8), :] = cells8.astype(BF)


def half_of(tile):
    return (tile // 2) % 2


def place_of(tile):
    return (tile // 4) * 2 + tile % 2


def take_slots(recv_ref, pos, seam_ref, corner_ref):
    rows = lax.broadcasted_iota(jnp.int32, (S, S), 0)
    cols = lax.broadcasted_iota(jnp.int32, (S, S), 1)
    strips = []
    for e in range(4):
        code = seam_ref[e, pos]
        tile = code // 8
        target = jnp.where(code % 2 == 1, S - 1 - rows, rows)
        turn = (cols == target).astype(F32).astype(BF)
        strip = recv_ref[place_of(tile), pl.ds(pl.multiple_of(S * half_of(tile), S), S), :]
        strips.append(jnp.dot(turn, strip, preferred_element_type=F32))
    cells = []
    row8 = lax.broadcasted_iota(jnp.int32, (SLOT - 2 * S, C), 0)
    for k in range(4):
        code = corner_ref[k, pos]
        tile = code // 4
        block = recv_ref[place_of(tile), pl.ds(2 * S, SLOT - 2 * S), :].astype(F32)
        row = 4 * half_of(tile) + code % 4
        cells.append(jnp.sum(jnp.where(row8 == row, block, 0.0), axis=0, keepdims=True))
    return strips, cells


def edge_kernel(waits, field_ref, out_ref, wide_ref):
    wide_ref[...] = field_ref[...].astype(F32)
    strips = [wide_ref[0], wide_ref[S - 1], wide_ref[:, 0, :], wide_ref[:, S - 1, :]]
    cells = [wide_ref[i, pl.ds(j, 1), :] for i in (0, S - 1) for j in (0, S - 1)]
    put_edges(out_ref, strips, cells)


def slot_kernel(waits, pos_ref, seam_ref, own_ref, other_ref, out_ref):
    pos = pos_ref[0]
    half = half_of(pos)
    mine = own_ref[pl.ds(4 * S, 8), :].astype(F32)
    other = other_ref[pl.ds(4 * S, 8), :].astype(F32)
    row8 = lax.broadcasted_iota(jnp.int32, (8, C), 0)
    first = jnp.where(half == 0, mine, other)
    second = jnp.where(half == 0, other, mine)
    cells8 = jnp.where(row8 < 4, first, pltpu.roll(second, 4, 0)).astype(BF)

    def put(p, carry):
        out_ref[p, pl.ds(2 * S, SLOT - 2 * S), :] = cells8
        return carry

    lax.fori_loop(0, 32, put, 0)
    for source, edges, at_half in ((pos, own_ref, half), (pos ^ 2, other_ref, 1 - half)):
        for e in range(4):
            tile = seam_ref[e, source] // 8

            @pl.when(half_of(tile) == half)
            def _(tile=tile, edges=edges, at_half=at_half, e=e):
                rows = pl.ds(pl.multiple_of(S * at_half, S), S)
                out_ref[place_of(tile), rows, :] = edges[pl.ds(S * e, S), :]


def mlp_rows(normed, cot, out, gain_parts, w_in_ref, b_in_ref, w_out_ref, keep):
    gain, xhat, istd = gain_parts
    dnorm = jnp.zeros(out.shape, F32)
    sums = []
    for n in range(4):
        h = slice(256 * n, 256 * n + 256)
        z = jnp.dot(normed, w_in_ref[:, h], preferred_element_type=F32) + b_in_ref[:, h]
        dact = lax.dot_general(
            cot, w_out_ref[h, :], (((1,), (1,)), ((), ())), preferred_element_type=F32
        )
        z2 = z * z
        half = 0.5 + 0.5 * jnp.tanh(z * (GELU_C + (GELU_C * 0.044715) * z2))
        act = z * half
        slope = half + act * (1.0 - half) * (2 * GELU_C + (6 * GELU_C * 0.044715) * z2)
        act = act.astype(BF)
        dhid = (dact * slope).astype(BF)
        keep(n, act, dhid)
        sums.append(jnp.sum(dhid.astype(F32), axis=0, keepdims=True))
        out = out + jnp.dot(act, w_out_ref[h, :], preferred_element_type=F32)
        dnorm = dnorm + lax.dot_general(
            dhid, w_in_ref[:, h], (((1,), (1,)), ((), ())), preferred_element_type=F32
        )
    dunit = dnorm * gain
    dconv = istd * (
        dunit
        - jnp.mean(dunit, axis=1, keepdims=True)
        - xhat * jnp.mean(dunit * xhat, axis=1, keepdims=True)
    )
    sums.append(jnp.sum(dnorm * xhat, axis=0, keepdims=True))
    sums.append(jnp.sum(dnorm, axis=0, keepdims=True))
    return out.astype(BF), dconv.astype(BF).astype(F32), sums


def norm_rows(rows):
    centred = rows - jnp.mean(rows, axis=1, keepdims=True)
    istd = 1.0 / jnp.sqrt(jnp.mean(centred * centred, axis=1, keepdims=True) + 1e-06)
    return centred * istd, istd


OVER_ROWS = (((0,), (0,)), ((), ()))


def inside_kernel(
    waits,
    field_ref,
    cot_ref,
    kern_ref,
    bias_ref,
    gain_ref,
    shift_ref,
    b_out_ref,
    w_in_ref,
    b_in_ref,
    w_out_ref,
    blocks_ref,
    base_ref,
    grad_ref,
    pad_ref,
    xhat_ref,
    istd_ref,
    normed_ref,
    active_ref,
    dhid_ref,
    keep_ref,
    dconv_ref,
):
    center = field_ref[...].astype(F32)
    pad_ref[:, 0] = jnp.zeros((3, S, C), F32)
    pad_ref[:, S + 1] = jnp.zeros((3, S, C), F32)
    pad_ref[1, pl.ds(1, S)] = center
    pad_ref[0, pl.ds(1, S)] = pltpu.roll(center, 1, 1)
    pad_ref[2, pl.ds(1, S)] = pltpu.roll(center, S - 1, 1)

    bias = bias_ref[...]
    gain = gain_ref[...]
    shift = shift_ref[...]
    b_out = b_out_ref[...]
    rowid = lax.broadcasted_iota(jnp.int32, (256, C), 0)
    col = rowid & (S - 1)

    def forward_rows(b, carry):
        r0 = b * 8
        acc = jnp.zeros((8, S, C), F32) + bias.reshape(1, 1, C)
        for u in range(3):
            for v in range(3):
                k = 3 * u + v
                acc = acc + pad_ref[v, pl.ds(r0 + u, 8)] * kern_ref[k : k + 1, :].reshape(1, 1, C)
        xhat, istd = norm_rows(acc.reshape(8 * S, C))
        q = pl.ds(pl.multiple_of(b * 256, 256), 256)
        xhat_ref[q, :] = xhat
        istd_ref[q, :] = jnp.broadcast_to(istd, (256, 128))
        normed_ref[q, :] = (xhat * gain + shift).astype(BF)
        row = r0 + (rowid >> 5)
        kept = (col > 0) & (col < S - 1) & (row > 0) & (row < S - 1)
        keep_ref[q, :] = jnp.where(kept, cot_ref[q, :].astype(F32), 0.0).astype(BF)
        return carry

    lax.fori_loop(0, 4, forward_rows, 0)
    waits[7]()
    waits[9]()

    def block_rows(b, carry):
        q = pl.ds(pl.multiple_of(b * 256, 256), 256)

        def keep(n, act, dhid):
            active_ref[q, 256 * n : 256 * n + 256] = act
            dhid_ref[q, 256 * n : 256 * n + 256] = dhid

        out = field_ref[pl.ds(b * 8, 8)].reshape(256, C).astype(F32) + b_out
        parts = (gain, xhat_ref[q, :], istd_ref[q, 0:1])
        out, dconv, sums = mlp_rows(
            normed_ref[q, :], keep_ref[q, :], out, parts, w_in_ref, b_in_ref, w_out_ref, keep
        )
        blocks_ref[q, :] = out
        dconv_ref[pl.ds(b * 8, 8)] = dconv.reshape(8, S, C)
        sums.append(jnp.sum(cot_ref[q, :].astype(F32), axis=0, keepdims=True))
        return tuple(a + x for a, x in zip(carry, sums))

    zero = jnp.zeros((1, C), F32)
    *g_bin, g_gain, g_shift, g_bout = lax.fori_loop(0, 4, block_rows, (zero,) * 7)

    for n in range(4):
        h = slice(256 * n, 256 * n + 256)
        dot = functools.partial(lax.dot_general, dimension_numbers=OVER_ROWS, preferred_element_type=F32)
        g = dot(normed_ref[...], dhid_ref[:, h])
        grad_ref[4 * n : 4 * n + 4, pl.ds(0, 64), :] = g.reshape(4, 64, C)
        g = dot(active_ref[:, h], keep_ref[...])
        grad_ref[16 + 4 * n : 20 + 4 * n, pl.ds(0, 64), :] = g.reshape(4, 64, C)

    g_kernel = []
    for u in range(3):
        for v in range(3):

            def tap_rows(b, acc, u=u, v=v):
                part = pad_ref[v, pl.ds(b * 4 + u, 4)] * dconv_ref[pl.ds(b * 4, 4)]
                return acc + jnp.sum(part.reshape(4 * S // 8, 8, C), axis=0)

            acc = lax.fori_loop(0, 8, tap_rows, jnp.zeros((8, C), F32))
            g_kernel.append(jnp.sum(acc, axis=0, keepdims=True))

    def bias_rows(b, acc):
        return acc + jnp.sum(dconv_ref[pl.ds(b * 4, 4)].reshape(4 * S // 8, 8, C), axis=0)

    g_bias = jnp.sum(lax.fori_loop(0, 8, bias_rows, jnp.zeros((8, C), F32)), axis=0, keepdims=True)

    small = g_kernel + [g_bias, g_gain, g_shift, g_bout] + g_bin + [zero] * 15
    row8 = lax.broadcasted_iota(jnp.int32, (CHUNK - 64, C), 0)
    for j in range(32):
        grad_ref[j, pl.ds(64, CHUNK - 64), :] = jnp.where(row8 == 0, small[j], 0.0)

    def shift_rows(i, carry):
        row = dconv_ref[i]
        pad_ref[1, i + 1] = row
        pad_ref[0, i + 1] = pltpu.roll(row, S - 1, 0)
        pad_ref[2, i + 1] = pltpu.roll(row, 1, 0)
        return carry

    lax.fori_loop(0, S, shift_rows, 0)
    taps = [kern_ref[k : k + 1, :].reshape(1, 1, C) for k in range(9)]

    def inner_rows(b, carry):
        q = pl.ds(pl.multiple_of(b * 4 * S, 4 * S), 4 * S)
        acc = cot_ref[q, :].astype(F32).reshape(4, S, C)
        for u in range(3):
            for v in range(3):
                acc = acc + pad_ref[v, pl.ds(b * 4 + 2 - u, 4)] * taps[3 * u + v]
        base_ref[pl.ds(b * 4, 4)] = acc
        return carry

    lax.fori_loop(0, 8, inner_rows, 0)


def border_kernel(
    waits,
    pos_ref,
    seam_ref,
    corner_ref,
    field_ref,
    cot_ref,
    recv_ref,
    kern_ref,
    bias_ref,
    gain_ref,
    shift_ref,
    b_out_ref,
    w_in_ref,
    b_in_ref,
    w_out_ref,
    grad_ref,
    rows_ref,
    lines_ref,
    rim_ref,
    own_ref,
    send_ref,
    wide_ref,
):
    pos = pos_ref[0]
    core = pos % 2
    strips, cells = take_slots(recv_ref, pos, seam_ref, corner_ref)
    top, bottom, left, right = strips
    last = S - 1
    wide_ref[...] = field_ref[...].astype(F32)
    at_row = lambda i: wide_ref[i]
    at_col = lambda j: wide_ref[:, j, :]
    spot = lambda line, i: line[i : i + 1]
    place = lax.broadcasted_iota(jnp.int32, (S, C), 0)
    flat = lambda k: kern_ref[k : k + 1, :]

    bands = [
        (
            (top, at_row(0), at_row(1)),
            ((cells[0], cells[1]), (spot(left, 0), spot(right, 0)), (spot(left, 1), spot(right, 1))),
            lambda a, s: 3 * a + s,
        ),
        (
            (bottom, at_row(last), at_row(last - 1)),
            (
                (cells[2], cells[3]),
                (spot(left, last), spot(right, last)),
                (spot(left, last - 1), spot(right, last - 1)),
            ),
            lambda a, s: 3 * (2 - a) + s,
        ),
        (
            (left, at_col(0), at_col(1)),
            ((cells[0], cells[2]), (spot(top, 0), spot(bottom, 0)), (spot(top, 1), spot(bottom, 1))),
            lambda a, s: 3 * s + a,
        ),
        (
            (right, at_col(last), at_col(last - 1)),
            (
                (cells[1], cells[3]),
                (spot(top, last), spot(bottom, last)),
                (spot(top, last - 1), spot(bottom, last - 1)),
            ),
            lambda a, s: 3 * s + 2 - a,
        ),
    ]
    windows = [[None] * 9 for _ in range(4)]
    rows = []
    for n, (lines, ends, tap) in enumerate(bands):
        acc = jnp.zeros((S, C), F32) + bias_ref[...]
        for a in range(3):
            before = jnp.where(place == 0, ends[a][0], pltpu.roll(lines[a], 1, 0))
            after = jnp.where(place == last, ends[a][1], pltpu.roll(lines[a], last, 0))
            for s, window in enumerate((before, lines[a], after)):
                k = tap(a, s)
                windows[n][k] = window
                acc = acc + window * flat(k)
        rows.append(acc)
    field_rows = jnp.concatenate([lines[1] for lines, _, _ in bands], axis=0)
    wide_ref[...] = cot_ref[...].astype(F32)
    once = (place > 0) & (place < last)
    cot_rows = jnp.concatenate(
        [at_row(0), at_row(last)]
        + [jnp.where(once, at_col(0), 0.0), jnp.where(once, at_col(last), 0.0)],
        axis=0,
    ).astype(BF)

    gain = gain_ref[...]
    waits[11]()
    waits[13]()
    xhat, istd = norm_rows(jnp.concatenate(rows, axis=0))
    normed = (xhat * gain + shift_ref[...]).astype(BF)
    kept = []
    out, dconv, sums = mlp_rows(
        normed,
        cot_rows,
        field_rows + b_out_ref[...],
        (gain, xhat, istd),
        w_in_ref,
        b_in_ref,
        w_out_ref,
        lambda n, act, dhid: kept.append((act, dhid)),
    )
    rows_ref[...] = out
    *g_bin, g_gain, g_shift = sums
    d_lines = [dconv[S * n : S * n + S] for n in range(4)]

    def spread(line, taps):
        back = jnp.where(place == last, 0.0, pltpu.roll(line, last, 0))
        ahead = jnp.where(place == 0, 0.0, pltpu.roll(line, 1, 0))
        return back * flat(taps[0]) + line * flat(taps[1]) + ahead * flat(taps[2])

    def whole(line, at):
        line = jnp.where(place == 0, spot(d_lines[0], at), line)
        return jnp.where(place == last, spot(d_lines[1], at), line)

    row_taps = lambda u: (3 * u, 3 * u + 1, 3 * u + 2)
    col_taps = lambda v: (v, 3 + v, 6 + v)
    rim = [
        spread(d_lines[0], row_taps(0)),
        spread(d_lines[1], row_taps(2)),
        spread(whole(d_lines[2], 0), col_taps(0)),
        spread(whole(d_lines[3], last), col_taps(2)),
    ]
    corners = [
        spot(d_lines[0], 0) * flat(0),
        spot(d_lines[0], last) * flat(2),
        spot(d_lines[1], 0) * flat(6),
        spot(d_lines[1], last) * flat(8),
    ]
    put_edges(rim_ref, rim, corners)
    lines_ref[0] = spread(d_lines[0], row_taps(1))
    lines_ref[1] = spread(d_lines[0], row_taps(2))
    lines_ref[2] = spread(d_lines[1], row_taps(0))
    lines_ref[3] = spread(d_lines[1], row_taps(1))
    lines_ref[4] = spread(d_lines[2], col_taps(1))
    lines_ref[5] = spread(d_lines[2], col_taps(2))
    lines_ref[6] = spread(d_lines[3], col_taps(0))
    lines_ref[7] = spread(d_lines[3], col_taps(1))

    waits[14]()

    def put_rows(first, value):
        mine = core == first // 16
        base = first % 16
        value = value.reshape(4, 64, C) + grad_ref[first : first + 4, pl.ds(0, 64), :]

        @pl.when(mine)
        def _():
            own_ref[pl.ds(base, 4), pl.ds(0, 64), :] = value.astype(BF)

        @pl.when(jnp.logical_not(mine))
        def _():
            send_ref[pl.ds(base, 4), pl.ds(0, 64), :] = value.astype(BF)

    for n in range(4):
        act, dhid = kept[n]
        put_rows(4 * n, lax.dot_general(normed, dhid, OVER_ROWS, preferred_element_type=F32))
        put_rows(16 + 4 * n, lax.dot_general(act, cot_rows, OVER_ROWS, preferred_element_type=F32))

    g_kernel = []
    for k in range(9):
        acc = sum(windows[n][k] * d_lines[n] for n in range(4))
        g_kernel.append(jnp.sum(acc, axis=0, keepdims=True))
    zero = jnp.zeros((1, C), F32)
    g_bias = jnp.sum(dconv, axis=0, keepdims=True)
    small = g_kernel + [g_bias, g_gain, g_shift, zero] + g_bin + [zero] * 15
    row8 = lax.broadcasted_iota(jnp.int32, (CHUNK - 64, C), 0)
    for j in range(32):
        row = jnp.where(row8 == 0, small[j], 0.0) + grad_ref[j, pl.ds(64, CHUNK - 64), :]

        @pl.when(core == j // 16)
        def _(row=row, j=j):
            own_ref[j % 16, pl.ds(64, CHUNK - 64), :] = row.astype(BF)

        @pl.when(core != j // 16)
        def _(row=row, j=j):
            send_ref[j % 16, pl.ds(64, CHUNK - 64), :] = row.astype(BF)


def patch_kernel(waits, part_ref, rows_ref, blocks_ref, wide_ref):
    last = S - 1
    wide_ref[...] = part_ref[...].astype(F32)
    rows = rows_ref[...].astype(F32)
    wide_ref[:, 0, :] = rows[2 * S : 3 * S]
    wide_ref[:, last, :] = rows[3 * S : 4 * S]
    wide_ref[0] = rows[0:S]
    wide_ref[last] = rows[S : 2 * S]
    blocks_ref[...] = wide_ref[...].astype(BF)


def join_kernel(
    waits, pos_ref, seam_ref, corner_ref, base_ref, lines_ref, recv_ref, out_ref, acc_ref
):
    strips, cells = take_slots(recv_ref, pos_ref[0], seam_ref, corner_ref)
    last = S - 1
    acc_ref[...] = base_ref[...]
    for i, add in (
        (0, strips[0] + lines_ref[0]),
        (1, lines_ref[1]),
        (last - 1, lines_ref[2]),
        (last, strips[1] + lines_ref[3]),
    ):
        acc_ref[i] = acc_ref[i] + add
    for j, add in (
        (0, strips[2] + lines_ref[4]),
        (1, lines_ref[5]),
        (last - 1, lines_ref[6]),
        (last, strips[3] + lines_ref[7]),
    ):
        acc_ref[:, j, :] = acc_ref[:, j, :] + add
    for n, (i, j) in enumerate(((0, 0), (0, last), (last, 0), (last, last))):
        acc_ref[i, pl.ds(j, 1), :] = acc_ref[i, pl.ds(j, 1), :] + cells[n]
    out_ref[...] = acc_ref[...].astype(BF)


def scale_kernel(
    waits, at_ref, own_ref, other_ref, kern_ref, chan_ref, w_in_ref, b_in_ref, w_out_ref, entries
):
    core = at_ref[0] % 2
    halves = (own_ref, other_ref)
    sums = []
    for half in range(2):
        def one_half(j, acc, half=half):
            v = jnp.where(core == half, own_ref[j].astype(F32), other_ref[j].astype(F32))
            return acc + jnp.sum((v * v).reshape(CHUNK // 8, 8, C), axis=0)

        sums.append(lax.fori_loop(0, 16, one_half, jnp.zeros((8, C), F32)))
    total = jnp.sum(jnp.sum(sums[0] + sums[1], axis=0, keepdims=True), axis=1, keepdims=True)
    scale = 1.0 / jnp.sqrt(total / entries + 1e-06)

    for j in range(32):
        c, k = j // 16, j % 16

        def emit(ref, j=j, k=k):
            rows = ref[k, pl.ds(0, 64), :].astype(F32) * scale
            if j < 16:
                w_in_ref[64 * (j % 4) : 64 * (j % 4) + 64, 256 * (j // 4) : 256 * (j // 4) + 256] = rows
            else:
                w_out_ref[64 * (j - 16) : 64 * (j - 16) + 64, :] = rows
            row = ref[k, pl.ds(64, 8), :].astype(F32)[0:1] * scale
            if j < 9:
                kern_ref[j : j + 1, :] = row
            elif j < 13:
                chan_ref[j - 9 : j - 8, :] = row
            elif j < 17:
                b_in_ref[:, 256 * (j - 13) : 256 * (j - 13) + 256] = row

        for near in range(2):

            @pl.when((core == c) == (near == 1))
            def _(emit=emit, near=near):
                emit(halves[1 - near])


def at(y, x, h, c):
    return ((y * 4 + x) * 2 + h) * 2 + c


def moves(axis, d):
    pairs = []
    for y in range(4):
        for x in range(4):
            for h in range(2):
                for c in range(2):
                    to = {
                        "y": ((y + d) % 4, x, h, c),
                        "x": (y, (x + d) % 4, h, c),
                        "h": (y, x, 1 - h, c),
                        "c": (y, x, h, 1 - c),
                    }[axis]
                    pairs.append((at(y, x, h, c), at(*to)))
    return pairs


def exchange(slots):
    halves = [[at(p // 8, p // 2 % 4, h, p % 2) for p in range(32)] for h in range(2)]
    return lax.all_to_all(slots, "space", 0, 0, axis_index_groups=halves, tiled=True)


def plane(slots):
    planes = [
        [at(p % 4, p // 4, h, c) for p in range(16)] for h in range(2) for c in range(2)
    ]
    return lax.all_to_all(slots, "space", 0, 0, axis_index_groups=planes, tiled=True)


def sum_over_devices(own, send, slots):
    rest = own.astype(F32) + lax.ppermute(send, "space", moves("c", 1)).astype(F32)
    parts = plane(rest.astype(BF))
    piece = jnp.sum(parts.astype(F32), axis=0)
    piece, slots = lax.optimization_barrier((piece, slots))
    back = exchange(slots)
    mine = piece.astype(BF)
    other = lax.ppermute(mine, "space", moves("h", 1))
    piece = mine.astype(F32) + other.astype(F32)
    turn = lambda d: [(i, (i + d) % 4) for i in range(4)]
    mine = piece.astype(BF)
    got = [mine] + [lax.ppermute(mine, "batch", turn(d)) for d in (1, 2, 3)]
    got = [g.astype(F32) for g in got]
    piece = (got[0] + got[2]) + (got[1] + got[3])
    piece, back = lax.optimization_barrier((piece.astype(BF), back))
    full = plane(jnp.broadcast_to(piece[None], (16, CHUNK, C)))
    return full, lax.ppermute(full, "space", moves("c", 1)), back


def shards(
    fields,
    cotangent,
    dw_kernel,
    dw_bias,
    ln_gain,
    ln_shift,
    w_in,
    b_in,
    w_out,
    b_out,
    seam_links,
    corner_links,
):
    here = lax.axis_index("space").reshape(1)
    links, diagonals = seam_links.T, corner_links.T
    field = fields[0, 0]
    cot = cotangent[0, 0]
    sds = jax.ShapeDtypeStruct
    edges = sds((EDGE, C), BF)
    wide = pltpu.VMEM((S, S, C), F32)

    def to_slots(mine):
        other = lax.ppermute(mine, "space", moves("h", 1))
        return staged_call(
            slot_kernel,
            [(here, "smem", 0), (links, "smem", 0), (mine, "vmem", 0), (other, "vmem", 0)],
            [(sds((32, SLOT, C), BF), True)],
            [],
            63,
        )[0]

    (field_edges,) = staged_call(edge_kernel, [(field, "vmem", 0)], [(edges, True)], [wide], 63)
    halo = exchange(to_slots(field_edges))

    cells = S * S
    row = lambda v: (v.reshape(1, -1), "vmem", 0)
    weights = [
        (dw_kernel, "vmem", 0),
        row(dw_bias),
        row(ln_gain),
        row(ln_shift),
        row(b_out),
        (w_in, "vmem", 1),
        row(b_in),
        (w_out, "vmem", 1),
    ]
    part, base, grads = staged_call(
        inside_kernel,
        [(field, "vmem", 0), (cot.reshape(cells, C), "vmem", 0)] + weights,
        [
            (sds((cells, C), BF), True),
            (sds((S, S, C), F32), True),
            (sds((32, CHUNK, C), F32), True),
        ],
        [
            pltpu.VMEM((3, S + 2, S, C), F32),
            pltpu.VMEM((cells, C), F32),
            pltpu.VMEM((cells, 128), F32),
            pltpu.VMEM((cells, C), BF),
            pltpu.VMEM((cells, H), BF),
            pltpu.VMEM((cells, H), BF),
            pltpu.VMEM((cells, C), BF),
            wide,
        ],
        63,
        pl.CostEstimate(
            flops=12 * cells * C * H, bytes_accessed=8 << 20, transcendentals=cells * H
        ),
    )
    where = [(here, "smem", 0), (links, "smem", 0), (diagonals, "smem", 0)]
    border_rows, lines, rim, own, send = staged_call(
        border_kernel,
        where
        + [(field, "vmem", 0), (cot, "vmem", 0), (halo, "vmem", 0)]
        + weights
        + [(grads, "vmem", 1)],
        [
            (sds((4 * S, C), BF), True),
            (sds((8, S, C), F32), True),
            (edges, True),
            (sds((16, CHUNK, C), BF), True),
            (sds((16, CHUNK, C), BF), True),
        ],
        [wide],
        63,
    )
    (blocks,) = staged_call(
        patch_kernel,
        [(part.reshape(S, S, C), "vmem", 0), (border_rows, "vmem", 0)],
        [(sds((S, S, C), BF), True)],
        [wide],
        63,
    )
    near, far, back = sum_over_devices(own, send, to_slots(rim))
    (grad_tile,) = staged_call(
        join_kernel,
        where + [(base, "vmem", 0), (lines, "vmem", 0), (back, "here", 0)],
        [(sds((S, S, C), BF), True)],
        [wide],
        10,
    )
    entries = 13 * C + 2 * C * H + H
    grad_kernel, grad_channels, grad_w_in, grad_b_in, grad_w_out = staged_call(
        functools.partial(scale_kernel, entries=entries),
        [(here, "smem", 0), (near, "here", 0), (far, "here", 0)],
        [
            (sds((9, C), F32), True),
            (sds((4, C), F32), True),
            (sds((C, H), F32), True),
            (sds((1, H), F32), True),
            (sds((H, C), F32), True),
        ],
        [],
        10,
    )
    return (
        blocks[None, None],
        grad_tile[None, None],
        grad_kernel,
        grad_channels,
        grad_w_in,
        grad_b_in.reshape(H),
        grad_w_out,
    )


def solution(mesh):
    tile = P("batch", "space", None, None, None)

    return jax.shard_map(
        shards,
        mesh=mesh,
        in_specs=(tile, tile) + (P(),) * 10,
        out_specs=(tile, tile) + (P(),) * 5,
        check_vma=False,
    )
```

profile of v0, /device:TPU:1, one launch (start us, length us, event | category | flops | bytes accessed | tf_op | source)
XLA Modules:
  0.0 124.3 jit_solution(5313404212017387690)
XLA Ops:
  0.6 1.8 %shard_map.172.refs_2_ = bf16[136,256]{1,0:T(8,128)(2,1)} custom-call(bf16[32,32,256]{2,1,0:T(8,128)(2,1)} %bitcast.21), custom_call_target="tpu_custom_call" | custom-call | tf_op jit(solution)/shard_map/pallas_call | solution.py:66
  2.5 7.8 %collective-permute-start = (bf16[136,256]{1,0:T(8,128)(2,1)}, bf16[136,256]{1,0:T(8,128)(2,1)S(1)}, u32[]{:S(2)}, u32[]{:S(2)}) collective-permute-start(bf16[136,256]{1,0:T(8,128)(2,1)} %shard_map.172.refs_2_), channel_id=1, source_target_pairs={{0,8},{4,12},{8,0},{12,4},{16,24},{20,28},{24,16},{28,20},{32,40},... | collective-permute-start | bytes 208904 | tf_op jit(solution)/shard_map/ppermute | solution.py:650
  10.3 2.0 %collective-permute-done.refs_3_ = bf16[136,256]{1,0:T(8,128)(2,1)S(1)} collective-permute-done((bf16[136,256]{1,0:T(8,128)(2,1)}, bf16[136,256]{1,0:T(8,128)(2,1)S(1)}, u32[]{:S(2)}, u32[]{:S(2)}) %collective-permute-start) | collective-permute-done | bytes 69664 | tf_op jit(solution)/shard_map/ppermute | solution.py:650
  12.3 0.0 copy-start.7
  12.3 0.6 copy-done.7
  12.9 2.4 %shard_map.173 = bf16[32,72,256]{2,1,0:T(8,128)(2,1)} custom-call(s32[1]{0:T(128)} %bitcast.8.refs_0_, s32[4,64]{1,0:T(4,128)} %bitcast.15, bf16[136,256]{1,0:T(8,128)(2,1)} %shard_map.172.refs_2_, bf16[136,256]{1,0:T(8,128)(2,1)} %copy-done.7), custom_call_target="tpu_custom_call" | custom-call | tf_op jit(solution)/shard_map/pallas_call | solution.py:66
  15.3 9.0 %all-to-all-start = ((bf16[32,72,256]{2,1,0:T(8,128)(2,1)}), bf16[32,72,256]{2,1,0:T(8,128)(2,1)}, u32[]{:S(2)}, u32[]{:S(2)}) async-start(bf16[32,72,256]{2,1,0:T(8,128)(2,1)} %shard_map.173), calls=%async_computation | async-start | bytes 2359296 | tf_op jit(solution)/shard_map/all_to_all | solution.py:598
  24.3 14.5 %shard_map.171 = (bf16[1024,256]{1,0:T(8,128)(2,1)}, f32[32,32,256]{2,1,0:T(8,128)}, f32[32,72,256]{2,1,0:T(8,128)}) custom-call(bf16[32,32,256]{2,1,0:T(8,128)(2,1)} %bitcast.22, bf16[1024,256]{1,0:T(8,128)(2,1)} %bitcast.24, f32[9,256]{1,0:T(8,128)} %refs_6_.1, f32[1,256]{1,0:T(1,128)} %bitcast.31, f32[1,256]{1,0:T(1,128)} %bitcast.33, f32[1,256]{1,0:T(1,128)} %bitcast.35, ...), custom_call_target="tpu_custom_call" | custom-call | flops 3221225472 | bytes 8388608 | tf_op jit(solution)/shard_map/pallas_call | solution.py:66
  38.9 4.1 %all-to-all-done.refs_5_ = bf16[32,72,256]{2,1,0:T(8,128)(2,1)} async-done(((bf16[32,72,256]{2,1,0:T(8,128)(2,1)}), bf16[32,72,256]{2,1,0:T(8,128)(2,1)}, u32[]{:S(2)}, u32[]{:S(2)}) %all-to-all-start) | async-done | bytes 1179680 | tf_op jit(solution)/shard_map/all_to_all | solution.py:598
  42.9 6.7 %shard_map.174 = (bf16[128,256]{1,0:T(8,128)(2,1)}, f32[8,32,256]{2,1,0:T(8,128)}, bf16[136,256]{1,0:T(8,128)(2,1)}, bf16[16,72,256]{2,1,0:T(8,128)(2,1)}, bf16[16,72,256]{2,1,0:T(8,128)(2,1)}) custom-call(s32[1]{0:T(128)} %bitcast.8.refs_0_, s32[4,64]{1,0:T(4,128)} %bitcast.16, s32[4,64]{1,0:T(4,128)} %bitcast.19, bf16[32,32,256]{2,1,0:T(8,128)(2,1)} %bitcast.23, ...), custom_call_target="tpu_custom_call" | custom-call | tf_op jit(solution)/shard_map/pallas_call | solution.py:66
  49.7 0.5 collective-permute-start.1
  50.2 1.8 %collective-permute-done.1 = bf16[16,72,256]{2,1,0:T(8,128)(2,1)S(1)} collective-permute-done((bf16[16,72,256]{2,1,0:T(8,128)(2,1)}, bf16[16,72,256]{2,1,0:T(8,128)(2,1)S(1)}, u32[]{:S(2)}, u32[]{:S(2)}) %collective-permute-start.1) | collective-permute-done | bytes 589856 | tf_op jit(solution)/shard_map/ppermute | solution.py:609
  52.0 0.0 copy-start.6
  52.0 2.1 %add_convert_fusion = bf16[16,72,256]{2,1,0:T(8,128)(2,1)} fusion(bf16[16,72,256]{2,1,0:T(8,128)(2,1)S(1)} %collective-permute-done.1, bf16[16,72,256]{2,1,0:T(8,128)(2,1)} %get-tuple-element.29), kind=kLoop, calls=%fused_computation.1 | loop fusion | flops 1179648 | bytes 1769472 | tf_op jit(solution)/shard_map/convert_element_type | solution.py:610
  54.1 3.6 %all-to-all-start.1 = ((bf16[16,72,256]{2,1,0:T(8,128)(2,1)}), bf16[16,72,256]{2,1,0:T(8,128)(2,1)S(1)}, u32[]{:S(2)}, u32[]{:S(2)}) async-start(bf16[16,72,256]{2,1,0:T(8,128)(2,1)} %add_convert_fusion), calls=%async_computation.1 | async-start | bytes 1179648 | tf_op jit(solution)/shard_map/all_to_all | solution.py:605
  57.7 0.0 copy-done.6
  57.7 6.1 %collective-permute-start.2 = (bf16[136,256]{1,0:T(8,128)(2,1)S(1)}, bf16[136,256]{1,0:T(8,128)(2,1)S(1)}, u32[]{:S(2)}, u32[]{:S(2)}) collective-permute-start(bf16[136,256]{1,0:T(8,128)(2,1)S(1)} %copy-done.6), channel_id=1, source_target_pairs={{0,8},{4,12},{8,0},{12,4},{16,24},{20,28},{24,16},{28,20},{32,40},... | collective-permute-start | bytes 208904 | tf_op jit(solution)/shard_map/ppermute | solution.py:650
  63.7 2.2 %collective-permute-done.2.refs_3_ = bf16[136,256]{1,0:T(8,128)(2,1)S(1)} collective-permute-done((bf16[136,256]{1,0:T(8,128)(2,1)S(1)}, bf16[136,256]{1,0:T(8,128)(2,1)S(1)}, u32[]{:S(2)}, u32[]{:S(2)}) %collective-permute-start.2) | collective-permute-done | bytes 69664 | tf_op jit(solution)/shard_map/ppermute | solution.py:650
  65.9 0.6 copy-done.8
  66.5 2.4 %shard_map.176 = bf16[32,72,256]{2,1,0:T(8,128)(2,1)} custom-call(s32[1]{0:T(128)} %bitcast.8.refs_0_, s32[4,64]{1,0:T(4,128)} %bitcast.17, bf16[136,256]{1,0:T(8,128)(2,1)} %get-tuple-element.31.refs_2_, bf16[136,256]{1,0:T(8,128)(2,1)} %copy-done.8), custom_call_target="tpu_custom_call" | custom-call | tf_op jit(solution)/shard_map/pallas_call | solution.py:66
  68.9 0.0 all-to-all-done.1
  69.0 0.1 convert_reduce_fusion
  69.0 8.8 %all-to-all-start.2 = ((bf16[32,72,256]{2,1,0:T(8,128)(2,1)}), bf16[32,72,256]{2,1,0:T(8,128)(2,1)S(1)}, u32[]{:S(2)}, u32[]{:S(2)}) async-start(bf16[32,72,256]{2,1,0:T(8,128)(2,1)} %shard_map.176), calls=%async_computation.2 | async-start | bytes 2359296 | tf_op jit(solution)/shard_map/all_to_all | solution.py:598
  77.8 6.2 %collective-permute-start.3 = (bf16[72,256]{1,0:T(8,128)(2,1)S(1)}, bf16[72,256]{1,0:T(8,128)(2,1)S(1)}, u32[]{:S(2)}, u32[]{:S(2)}) collective-permute-start(bf16[72,256]{1,0:T(8,128)(2,1)S(1)} %convert_reduce_fusion), channel_id=1, source_target_pairs={{0,8},{4,12},{8,0},{12,4},{16,24},{20,28},{24,16},{28,20},{32,40},... | collective-permute-start | bytes 110600 | tf_op jit(solution)/shard_map/ppermute | solution.py:615
  84.0 1.5 %collective-permute-done.3 = bf16[72,256]{1,0:T(8,128)(2,1)S(1)} collective-permute-done((bf16[72,256]{1,0:T(8,128)(2,1)S(1)}, bf16[72,256]{1,0:T(8,128)(2,1)S(1)}, u32[]{:S(2)}, u32[]{:S(2)}) %collective-permute-start.3) | collective-permute-done | bytes 36896 | tf_op jit(solution)/shard_map/ppermute | solution.py:615
  85.4 1.0 collective-permute-start.6
  86.5 1.2 collective-permute-start.5
  87.7 2.3 %collective-permute-start.4 = (bf16[72,256]{1,0:T(8,128)(2,1)S(1)}, bf16[72,256]{1,0:T(8,128)(2,1)S(1)}, u32[]{:S(2)}, u32[]{:S(2)}) collective-permute-start(bf16[72,256]{1,0:T(8,128)(2,1)S(1)} %add_convert_fusion.2), channel_id=1, source_target_pairs={{0,2},{1,3},{2,0},{3,1},{4,6},{5,7},{6,4},{7,5},{8,10},{9,11},{10,... | collective-permute-start | bytes 110600 | tf_op jit(solution)/shard_map/ppermute | solution.py:619
  90.0 0.0 collective-permute-done.6
  90.0 1.7 %collective-permute-done.5 = bf16[72,256]{1,0:T(8,128)(2,1)S(1)} collective-permute-done((bf16[72,256]{1,0:T(8,128)(2,1)S(1)}, bf16[72,256]{1,0:T(8,128)(2,1)S(1)}, u32[]{:S(2)}, u32[]{:S(2)}) %collective-permute-start.5) | collective-permute-done | bytes 36896 | tf_op jit(solution)/shard_map/ppermute | solution.py:619
  91.8 0.6 collective-permute-done.4
  92.4 4.0 %all-to-all-done.2.refs_5_ = bf16[32,72,256]{2,1,0:T(8,128)(2,1)S(1)} async-done(((bf16[32,72,256]{2,1,0:T(8,128)(2,1)}), bf16[32,72,256]{2,1,0:T(8,128)(2,1)S(1)}, u32[]{:S(2)}, u32[]{:S(2)}) %all-to-all-start.2) | async-done | bytes 1179680 | tf_op jit(solution)/shard_map/all_to_all | solution.py:598
  96.3 1.0 copy-done
  97.4 0.0 copy-start.3
  97.4 0.0 copy-start.4
  97.4 0.0 copy-start.5
  97.5 13.8 %all_to_all.20.refs_1_ = bf16[16,72,256]{2,1,0:T(8,128)(2,1)S(1)} all-to-all(bf16[16,72,256]{2,1,0:T(8,128)(2,1)S(1)} %broadcast_in_dim.14), channel_id=1, replica_groups={{0,64,128,192,16,80,144,208,32,96,160,224,48,112,176,240},{4,68,132,196..., dimensions={0} | all-to-all | bytes 1179648 | tf_op jit(solution)/shard_map/all_to_all | solution.py:605
  111.3 2.6 %collective-permute-start.7 = (bf16[16,72,256]{2,1,0:T(8,128)(2,1)S(1)}, bf16[16,72,256]{2,1,0:T(8,128)(2,1)}, u32[]{:S(2)}, u32[]{:S(2)}) collective-permute-start(bf16[16,72,256]{2,1,0:T(8,128)(2,1)S(1)} %all_to_all.20.refs_1_), channel_id=1, source_target_pairs={{0,4},{4,0},{8,12},{12,8},{16,20},{20,16},{24,28},{28,24},{32,36},... | collective-permute-start | bytes 1769480 | tf_op jit(solution)/shard_map/ppermute | solution.py:624
  113.8 2.0 %shard_map.175 = bf16[32,32,256]{2,1,0:T(8,128)(2,1)} custom-call(bf16[32,32,256]{2,1,0:T(8,128)(2,1)} %bitcast.27, bf16[128,256]{1,0:T(8,128)(2,1)} %get-tuple-element.26.refs_1_), custom_call_target="tpu_custom_call" | custom-call | tf_op jit(solution)/shard_map/pallas_call | solution.py:66
  115.9 0.0 copy-done.3
  115.9 0.0 copy-done.4
  115.9 0.0 copy-done.5
  115.9 0.0 copy-start.1
  115.9 1.3 %copy-done.1 = bf16[32,72,256]{2,1,0:T(8,128)(2,1)S(1)} copy-done((bf16[32,72,256]{2,1,0:T(8,128)(2,1)S(1)}, bf16[32,72,256]{2,1,0:T(8,128)(2,1)}, u32[]{:S(2)}) %copy-start.1) | copy-done | bytes 1179672
  117.2 1.2 copy-done.2
  118.4 1.8 %shard_map.177 = bf16[32,32,256]{2,1,0:T(8,128)(2,1)} custom-call(s32[1]{0:T(128)} %bitcast.8.refs_0_, s32[4,64]{1,0:T(4,128)S(1)} %bitcast.18, s32[4,64]{1,0:T(4,128)S(1)} %bitcast.20, f32[32,32,256]{2,1,0:T(8,128)S(1)} %copy-done.2, f32[8,32,256]{2,1,0:T(8,128)S(1)} %copy-done.3, bf16[32,72,256]{2,1,0:T(8,128)(2,1)S(1)} %copy-done.1), custom_call_target="tpu_custom_call" | custom-call | tf_op jit(solution)/shard_map/pallas_call | solution.py:66
  120.2 0.0 collective-permute-done.7.refs_2_
  120.2 4.1 %shard_map.178 = (f32[9,256]{1,0:T(8,128)}, f32[4,256]{1,0:T(4,128)}, f32[256,1024]{1,0:T(8,128)}, f32[1,1024]{1,0:T(1,128)}, f32[1024,256]{1,0:T(8,128)}) custom-call(s32[1]{0:T(128)} %bitcast.8.refs_0_, bf16[16,72,256]{2,1,0:T(8,128)(2,1)S(1)} %all_to_all.20.refs_1_, bf16[16,72,256]{2,1,0:T(8,128)(2,1)} %collective-permute-done.7.refs_2_), custom_call_target="tpu_custom_call" | custom-call | tf_op jit(solution)/shard_map/pallas_call | solution.py:66
  (6 shorter events, 0.1 us)
Async XLA Ops:
  2.5 9.8 %collective-permute-start = (bf16[136,256]{1,0:T(8,128)(2,1)}, bf16[136,256]{1,0:T(8,128)(2,1)S(1)}, u32[]{:S(2)}, u32[]{:S(2)}) collective-permute-start(bf16[136,256]{1,0:T(8,128)(2,1)} %shard_map.172.refs_2_), channel_id=1, source_target_pairs={{0,8},{4,12},{8,0},{12,4},{16,24},{20,28},{24,16},{28,20},{32,40},... | collective-permute-start | bytes 208904 | tf_op jit(solution)/shard_map/ppermute | solution.py:650
  12.3 0.6 copy-start.7
  15.3 27.6 %all-to-all-start = ((bf16[32,72,256]{2,1,0:T(8,128)(2,1)}), bf16[32,72,256]{2,1,0:T(8,128)(2,1)}, u32[]{:S(2)}, u32[]{:S(2)}) async-start(bf16[32,72,256]{2,1,0:T(8,128)(2,1)} %shard_map.173), calls=%async_computation | async-start | bytes 2359296 | tf_op jit(solution)/shard_map/all_to_all | solution.py:598
  49.7 2.3 %collective-permute-start.1 = (bf16[16,72,256]{2,1,0:T(8,128)(2,1)}, bf16[16,72,256]{2,1,0:T(8,128)(2,1)S(1)}, u32[]{:S(2)}, u32[]{:S(2)}) collective-permute-start(bf16[16,72,256]{2,1,0:T(8,128)(2,1)} %get-tuple-element.30), channel_id=1, source_target_pairs={{0,4},{4,0},{8,12},{12,8},{16,20},{20,16},{24,28},{28,24},{32,36},... | collective-permute-start | bytes 1769480 | tf_op jit(solution)/shard_map/ppermute | solution.py:609
  52.0 5.7 %copy-start.6 = (bf16[136,256]{1,0:T(8,128)(2,1)S(1)}, bf16[136,256]{1,0:T(8,128)(2,1)}, u32[]{:S(2)}) copy-start(bf16[136,256]{1,0:T(8,128)(2,1)} %get-tuple-element.31.refs_2_) | copy-start | bytes 208900
  54.1 14.9 %all-to-all-start.1 = ((bf16[16,72,256]{2,1,0:T(8,128)(2,1)}), bf16[16,72,256]{2,1,0:T(8,128)(2,1)S(1)}, u32[]{:S(2)}, u32[]{:S(2)}) async-start(bf16[16,72,256]{2,1,0:T(8,128)(2,1)} %add_convert_fusion), calls=%async_computation.1 | async-start | bytes 1179648 | tf_op jit(solution)/shard_map/all_to_all | solution.py:605
  57.7 8.2 %collective-permute-start.2 = (bf16[136,256]{1,0:T(8,128)(2,1)S(1)}, bf16[136,256]{1,0:T(8,128)(2,1)S(1)}, u32[]{:S(2)}, u32[]{:S(2)}) collective-permute-start(bf16[136,256]{1,0:T(8,128)(2,1)S(1)} %copy-done.6), channel_id=1, source_target_pairs={{0,8},{4,12},{8,0},{12,4},{16,24},{20,28},{24,16},{28,20},{32,40},... | collective-permute-start | bytes 208904 | tf_op jit(solution)/shard_map/ppermute | solution.py:650
  65.9 0.6 copy-start.8
  69.0 27.3 %all-to-all-start.2 = ((bf16[32,72,256]{2,1,0:T(8,128)(2,1)}), bf16[32,72,256]{2,1,0:T(8,128)(2,1)S(1)}, u32[]{:S(2)}, u32[]{:S(2)}) async-start(bf16[32,72,256]{2,1,0:T(8,128)(2,1)} %shard_map.176), calls=%async_computation.2 | async-start | bytes 2359296 | tf_op jit(solution)/shard_map/all_to_all | solution.py:598
  77.8 7.6 %collective-permute-start.3 = (bf16[72,256]{1,0:T(8,128)(2,1)S(1)}, bf16[72,256]{1,0:T(8,128)(2,1)S(1)}, u32[]{:S(2)}, u32[]{:S(2)}) collective-permute-start(bf16[72,256]{1,0:T(8,128)(2,1)S(1)} %convert_reduce_fusion), channel_id=1, source_target_pairs={{0,8},{4,12},{8,0},{12,4},{16,24},{20,28},{24,16},{28,20},{32,40},... | collective-permute-start | bytes 110600 | tf_op jit(solution)/shard_map/ppermute | solution.py:615
  85.4 4.6 %collective-permute-start.6 = (bf16[72,256]{1,0:T(8,128)(2,1)S(1)}, bf16[72,256]{1,0:T(8,128)(2,1)S(1)}, u32[]{:S(2)}, u32[]{:S(2)}) collective-permute-start(bf16[72,256]{1,0:T(8,128)(2,1)S(1)} %add_convert_fusion.2), channel_id=1, source_target_pairs={{0,3},{1,0},{2,1},{3,2},{4,7},{5,4},{6,5},{7,6},{8,11},{9,8},{10,9... | collective-permute-start | bytes 110600 | tf_op jit(solution)/shard_map/ppermute | solution.py:619
  86.5 5.3 %collective-permute-start.5 = (bf16[72,256]{1,0:T(8,128)(2,1)S(1)}, bf16[72,256]{1,0:T(8,128)(2,1)S(1)}, u32[]{:S(2)}, u32[]{:S(2)}) collective-permute-start(bf16[72,256]{1,0:T(8,128)(2,1)S(1)} %add_convert_fusion.2), channel_id=1, source_target_pairs={{0,1},{1,2},{2,3},{3,0},{4,5},{5,6},{6,7},{7,4},{8,9},{9,10},{10,1... | collective-permute-start | bytes 110600 | tf_op jit(solution)/shard_map/ppermute | solution.py:619
  87.7 4.7 %collective-permute-start.4 = (bf16[72,256]{1,0:T(8,128)(2,1)S(1)}, bf16[72,256]{1,0:T(8,128)(2,1)S(1)}, u32[]{:S(2)}, u32[]{:S(2)}) collective-permute-start(bf16[72,256]{1,0:T(8,128)(2,1)S(1)} %add_convert_fusion.2), channel_id=1, source_target_pairs={{0,2},{1,3},{2,0},{3,1},{4,6},{5,7},{6,4},{7,5},{8,10},{9,11},{10,... | collective-permute-start | bytes 110600 | tf_op jit(solution)/shard_map/ppermute | solution.py:619
  96.3 1.0 copy-start
  97.4 18.5 %copy-start.3 = (f32[8,32,256]{2,1,0:T(8,128)S(1)}, f32[8,32,256]{2,1,0:T(8,128)}, u32[]{:S(2)}) copy-start(f32[8,32,256]{2,1,0:T(8,128)} %get-tuple-element.28.refs_4_) | copy-start | bytes 786436
  97.4 18.5 %copy-start.4 = (s32[64,4]{0,1:T(4,128)S(1)}, s32[64,4]{0,1:T(4,128)}, u32[]{:S(2)}) copy-start(s32[64,4]{0,1:T(4,128)} %param.22) | copy-start | bytes 3076
  97.4 18.5 %copy-start.5 = (s32[64,4]{0,1:T(4,128)S(1)}, s32[64,4]{0,1:T(4,128)}, u32[]{:S(2)}) copy-start(s32[64,4]{0,1:T(4,128)} %param.23) | copy-start | bytes 3076
  111.3 8.9 %collective-permute-start.7 = (bf16[16,72,256]{2,1,0:T(8,128)(2,1)S(1)}, bf16[16,72,256]{2,1,0:T(8,128)(2,1)}, u32[]{:S(2)}, u32[]{:S(2)}) collective-permute-start(bf16[16,72,256]{2,1,0:T(8,128)(2,1)S(1)} %all_to_all.20.refs_1_), channel_id=1, source_target_pairs={{0,4},{4,0},{8,12},{12,8},{16,20},{20,16},{24,28},{28,24},{32,36},... | collective-permute-start | bytes 1769480 | tf_op jit(solution)/shard_map/ppermute | solution.py:624
  115.9 1.3 %copy-start.1 = (bf16[32,72,256]{2,1,0:T(8,128)(2,1)S(1)}, bf16[32,72,256]{2,1,0:T(8,128)(2,1)}, u32[]{:S(2)}) copy-start(bf16[32,72,256]{2,1,0:T(8,128)(2,1)} %copy-done) | copy-start | bytes 3538948
  117.2 1.2 copy-start.2
where the time goes:
time: 125 us; the launch traced here: 124 us
  starting transfers between devices  49 us (39%)
  Pallas kernels  35.8 us (29%)
  waiting for transfers between devices  17.9 us (14%)
  blocking collectives  13.8 us (11%)
  local copies, waits for them, and re-layouts  4.83 us (4%)
  other arithmetic  2.17 us (2%)
    pallas_call x8, Pallas kernels, staged_call(): pl.pallas_call(body, out_shape=tuple((o for o, _ in outs)), in_specs=[VME...  35.8 us
    all_to_all x2, starting transfers between devices, exchange(): lax.all_to_all(slots, 'space', 0, 0, axis_index_groups=halves, tiled=True)  17.8 us
    ppermute x2, starting transfers between devices, to_slots(): other = lax.ppermute(mine, 'space', moves('h', 1))  13.9 us
    all_to_all x1, blocking collectives, plane(): lax.all_to_all(slots, 'space', 0, 0, axis_index_groups=planes, tiled=True)  13.8 us
    all_to_all x2, waiting for transfers between devices, exchange(): lax.all_to_all(slots, 'space', 0, 0, axis_index_groups=halves, tiled=True)  8.05 us
    ppermute x1, starting transfers between devices, sum_over_devices(): other = lax.ppermute(mine, 'space', moves('h', 1))  6.16 us
    unnamed x18, local copies, waits for them, and re-layouts  4.79 us
    ppermute x3, starting transfers between devices, sum_over_devices(): got = [mine] + [lax.ppermute(mine, 'batch', turn(d)) for d in (1, 2, 3)]  4.57 us
  transfers between devices with their start and end apart: 11, of which 8 were waited for; matrix products, arithmetic and copies ran while one was open for 0% of the time, Pallas kernels for 17%

commit v1 on v0

--- a/solution.py
+++ b/solution.py
@@ -57,9 +57,17 @@
                 n += 1
             else:
                 args.append(ref)
+        started = []
+
+        def flush(i):
+            writes[i].start()
+            started.append(i)
+
+        waits["flush"] = flush
         kernel(waits, *args, *rest)
-        for copy in writes:
-            copy.start()
+        for i, copy in enumerate(writes):
+            if i not in started:
+                copy.start()
         for copy in writes:
             copy.wait()
 
@@ -336,8 +344,7 @@
     w_out_ref,
     grad_ref,
     rows_ref,
-    lines_ref,
-    rim_ref,
+    dconv_ref,
     own_ref,
     send_ref,
     wide_ref,
@@ -425,6 +432,55 @@
     *g_bin, g_gain, g_shift = sums
     d_lines = [dconv[S * n : S * n + S] for n in range(4)]
 
+    dconv_ref[...] = dconv
+
+    waits[14]()
+
+    def put_rows(first, value):
+        mine = core == first // 16
+        base = first % 16
+        value = value.reshape(4, 64, C) + grad_ref[first : first + 4, pl.ds(0, 64), :]
+
+        @pl.when(mine)
+        def _():
+            own_ref[pl.ds(base, 4), pl.ds(0, 64), :] = value
+
+        @pl.when(jnp.logical_not(mine))
+        def _():
+            send_ref[pl.ds(base, 4), pl.ds(0, 64), :] = value.astype(BF)
+
+    for n in range(4):
+        act, dhid = kept[n]
+        put_rows(4 * n, lax.dot_general(normed, dhid, OVER_ROWS, preferred_element_type=F32))
+        put_rows(16 + 4 * n, lax.dot_general(act, cot_rows, OVER_ROWS, preferred_element_type=F32))
+
+    g_kernel = []
+    for k in range(9):
+        acc = sum(windows[n][k] * d_lines[n] for n in range(4))
+        g_kernel.append(jnp.sum(acc, axis=0, keepdims=True))
+    zero = jnp.zeros((1, C), F32)
+    g_bias = jnp.sum(dconv, axis=0, keepdims=True)
+    small = g_kernel + [g_bias, g_gain, g_shift, zero] + g_bin + [zero] * 15
+    row8 = lax.broadcasted_iota(jnp.int32, (CHUNK - 64, C), 0)
+    for j in range(32):
+        row = jnp.where(row8 == 0, small[j], 0.0) + grad_ref[j, pl.ds(64, CHUNK - 64), :]
+
+        @pl.when(core == j // 16)
+        def _(row=row, j=j):
+            own_ref[j % 16, pl.ds(64, CHUNK - 64), :] = row
+
+        @pl.when(core != j // 16)
+        def _(row=row, j=j):
+            send_ref[j % 16, pl.ds(64, CHUNK - 64), :] = row.astype(BF)
+
+
+def rim_kernel(waits, dconv_ref, kern_ref, lines_ref, rim_ref):
+    last = S - 1
+    spot = lambda line, i: line[i : i + 1]
+    place = lax.broadcasted_iota(jnp.int32, (S, C), 0)
+    flat = lambda k: kern_ref[k : k + 1, :]
+    d_lines = [dconv_ref[S * n : S * n + S] for n in range(4)]
+
     def spread(line, taps):
         back = jnp.where(place == last, 0.0, pltpu.roll(line, last, 0))
         ahead = jnp.where(place == 0, 0.0, pltpu.roll(line, 1, 0))
@@ -458,45 +514,6 @@
     lines_ref[6] = spread(d_lines[3], col_taps(0))
     lines_ref[7] = spread(d_lines[3], col_taps(1))
 
-    waits[14]()
-
-    def put_rows(first, value):
-        mine = core == first // 16
-        base = first % 16
-        value = value.reshape(4, 64, C) + grad_ref[first : first + 4, pl.ds(0, 64), :]
-
-        @pl.when(mine)
-        def _():
-            own_ref[pl.ds(base, 4), pl.ds(0, 64), :] = value.astype(BF)
-
-        @pl.when(jnp.logical_not(mine))
-        def _():
-            send_ref[pl.ds(base, 4), pl.ds(0, 64), :] = value.astype(BF)
-
-    for n in range(4):
-        act, dhid = kept[n]
-        put_rows(4 * n, lax.dot_general(normed, dhid, OVER_ROWS, preferred_element_type=F32))
-        put_rows(16 + 4 * n, lax.dot_general(act, cot_rows, OVER_ROWS, preferred_element_type=F32))
-
-    g_kernel = []
-    for k in range(9):
-        acc = sum(windows[n][k] * d_lines[n] for n in range(4))
-        g_kernel.append(jnp.sum(acc, axis=0, keepdims=True))
-    zero = jnp.zeros((1, C), F32)
-    g_bias = jnp.sum(dconv, axis=0, keepdims=True)
-    small = g_kernel + [g_bias, g_gain, g_shift, zero] + g_bin + [zero] * 15
-    row8 = lax.broadcasted_iota(jnp.int32, (CHUNK - 64, C), 0)
-    for j in range(32):
-        row = jnp.where(row8 == 0, small[j], 0.0) + grad_ref[j, pl.ds(64, CHUNK - 64), :]
-
-        @pl.when(core == j // 16)
-        def _(row=row, j=j):
-            own_ref[j % 16, pl.ds(64, CHUNK - 64), :] = row.astype(BF)
-
-        @pl.when(core != j // 16)
-        def _(row=row, j=j):
-            send_ref[j % 16, pl.ds(64, CHUNK - 64), :] = row.astype(BF)
-
 
 def patch_kernel(waits, part_ref, rows_ref, blocks_ref, wide_ref):
     last = S - 1
@@ -551,6 +568,8 @@
 
     for j in range(32):
         c, k = j // 16, j % 16
+        if j == 16:
+            waits["flush"](2)
 
         def emit(ref, j=j, k=k):
             rows = ref[k, pl.ds(0, 64), :].astype(F32) * scale
@@ -606,10 +625,10 @@
 
 
 def sum_over_devices(own, send, slots):
-    rest = own.astype(F32) + lax.ppermute(send, "space", moves("c", 1)).astype(F32)
-    parts = plane(rest.astype(BF))
-    piece = jnp.sum(parts.astype(F32), axis=0)
-    piece, slots = lax.optimization_barrier((piece, slots))
+    other = lax.ppermute(send, "space", moves("c", 1))
+    rest = (own + other.astype(F32)).astype(BF)
+    parts = plane(rest)
+    piece = lax.optimization_barrier(jnp.sum(parts.astype(F32), axis=0))
     back = exchange(slots)
     mine = piece.astype(BF)
     other = lax.ppermute(mine, "space", moves("h", 1))
@@ -695,7 +714,7 @@
         ),
     )
     where = [(here, "smem", 0), (links, "smem", 0), (diagonals, "smem", 0)]
-    border_rows, lines, rim, own, send = staged_call(
+    border_rows, dconv, own, send = staged_call(
         border_kernel,
         where
         + [(field, "vmem", 0), (cot, "vmem", 0), (halo, "vmem", 0)]
@@ -703,12 +722,18 @@
         + [(grads, "vmem", 1)],
         [
             (sds((4 * S, C), BF), True),
-            (sds((8, S, C), F32), True),
-            (edges, True),
-            (sds((16, CHUNK, C), BF), True),
+            (sds((4 * S, C), F32), True),
+            (sds((16, CHUNK, C), F32), True),
             (sds((16, CHUNK, C), BF), True),
         ],
         [wide],
+        63,
+    )
+    lines, rim = staged_call(
+        rim_kernel,
+        [(dconv, "vmem", 0), (dw_kernel, "vmem", 0)],
+        [(sds((8, S, C), F32), True), (edges, True)],
+        [],
         63,
     )
     (blocks,) = staged_call(

time: 125 us -> 127 us (1.016)
  Pallas kernels: 35.8 us -> 37.3 us
    pallas_call x8 -> x9, Pallas kernels: 35.8 us -> 37.3 us  [staged_call(): pl.pallas_call(body, out_shape=tuple((o for o, _ in outs)), in_specs=[VME...]
    unnamed x18 -> x16, local copies, waits for them, and re-layouts: 4.79 us -> 4.8 us
  transfers between devices with their start and end apart: 11 -> 11, of which waited for: 8 -> 8; matrix products, arithmetic and copies ran while one was open for 0% -> 0% of each run, Pallas kernels for 17% -> 18%
where the time goes in v1:
time: 127 us; the launch traced here: 126 us
  starting transfers between devices  49 us (39%)
  Pallas kernels  37.3 us (29%)
  waiting for transfers between devices  18.1 us (14%)
  blocking collectives  13.8 us (11%)
  local copies, waits for them, and re-layouts  4.84 us (4%)
  other arithmetic  2.33 us (2%)
    pallas_call x9, Pallas kernels, staged_call(): pl.pallas_call(body, out_shape=tuple((o for o, _ in outs)), in_specs=[VME...  37.3 us
    all_to_all x2, starting transfers between devices, exchange(): lax.all_to_all(slots, 'space', 0, 0, axis_index_groups=halves, tiled=True)  17.9 us
    ppermute x2, starting transfers between devices, to_slots(): other = lax.ppermute(mine, 'space', moves('h', 1))  13.9 us
    all_to_all x1, blocking collectives, plane(): lax.all_to_all(slots, 'space', 0, 0, axis_index_groups=planes, tiled=True)  13.8 us
    all_to_all x2, waiting for transfers between devices, exchange(): lax.all_to_all(slots, 'space', 0, 0, axis_index_groups=halves, tiled=True)  8.06 us
    ppermute x1, starting transfers between devices, sum_over_devices(): other = lax.ppermute(mine, 'space', moves('h', 1))  6.06 us
    unnamed x16, local copies, waits for them, and re-layouts  4.8 us
    ppermute x3, starting transfers between devices, sum_over_devices(): got = [mine] + [lax.ppermute(mine, 'batch', turn(d)) for d in (1, 2, 3)]  4.57 us
  transfers between devices with their start and end apart: 11, of which 8 were waited for; matrix products, arithmetic and copies ran while one was open for 0% of the time, Pallas kernels for 18%

profile of v1, /device:TPU:1, one launch (start us, length us, event | category | flops | bytes accessed | tf_op | source)
XLA Modules:
  0.0 126.3 jit_solution(5264568663568513290)
XLA Ops:
  0.6 1.8 %shard_map.172.refs_2_ = bf16[136,256]{1,0:T(8,128)(2,1)} custom-call(bf16[32,32,256]{2,1,0:T(8,128)(2,1)} %bitcast.21), custom_call_target="tpu_custom_call" | custom-call | tf_op jit(solution)/shard_map/pallas_call | solution.py:74
  2.5 7.8 %collective-permute-start = (bf16[136,256]{1,0:T(8,128)(2,1)}, bf16[136,256]{1,0:T(8,128)(2,1)S(1)}, u32[]{:S(2)}, u32[]{:S(2)}) collective-permute-start(bf16[136,256]{1,0:T(8,128)(2,1)} %shard_map.172.refs_2_), channel_id=1, source_target_pairs={{0,8},{4,12},{8,0},{12,4},{16,24},{20,28},{24,16},{28,20},{32,40},... | collective-permute-start | bytes 208904 | tf_op jit(solution)/shard_map/ppermute | solution.py:669
  10.3 2.0 %collective-permute-done.refs_3_ = bf16[136,256]{1,0:T(8,128)(2,1)S(1)} collective-permute-done((bf16[136,256]{1,0:T(8,128)(2,1)}, bf16[136,256]{1,0:T(8,128)(2,1)S(1)}, u32[]{:S(2)}, u32[]{:S(2)}) %collective-permute-start) | collective-permute-done | bytes 69664 | tf_op jit(solution)/shard_map/ppermute | solution.py:669
  12.3 0.0 copy-start.6
  12.3 0.6 copy-done.6
  12.9 2.4 %shard_map.173 = bf16[32,72,256]{2,1,0:T(8,128)(2,1)} custom-call(s32[1]{0:T(128)} %bitcast.8.refs_0_, s32[4,64]{1,0:T(4,128)} %bitcast.15, bf16[136,256]{1,0:T(8,128)(2,1)} %shard_map.172.refs_2_, bf16[136,256]{1,0:T(8,128)(2,1)} %copy-done.6), custom_call_target="tpu_custom_call" | custom-call | tf_op jit(solution)/shard_map/pallas_call | solution.py:74
  15.3 9.0 %all-to-all-start = ((bf16[32,72,256]{2,1,0:T(8,128)(2,1)}), bf16[32,72,256]{2,1,0:T(8,128)(2,1)}, u32[]{:S(2)}, u32[]{:S(2)}) async-start(bf16[32,72,256]{2,1,0:T(8,128)(2,1)} %shard_map.173), calls=%async_computation | async-start | bytes 2359296 | tf_op jit(solution)/shard_map/all_to_all | solution.py:617
  24.3 14.5 %shard_map.171 = (bf16[1024,256]{1,0:T(8,128)(2,1)}, f32[32,32,256]{2,1,0:T(8,128)}, f32[32,72,256]{2,1,0:T(8,128)}) custom-call(bf16[32,32,256]{2,1,0:T(8,128)(2,1)} %bitcast.22, bf16[1024,256]{1,0:T(8,128)(2,1)} %bitcast.24, f32[9,256]{1,0:T(8,128)} %refs_1_.1, f32[1,256]{1,0:T(1,128)} %bitcast.31, f32[1,256]{1,0:T(1,128)} %bitcast.33, f32[1,256]{1,0:T(1,128)} %bitcast.35, ...), custom_call_target="tpu_custom_call" | custom-call | flops 3221225472 | bytes 8388608 | tf_op jit(solution)/shard_map/pallas_call | solution.py:74
  38.9 4.1 %all-to-all-done.refs_5_ = bf16[32,72,256]{2,1,0:T(8,128)(2,1)} async-done(((bf16[32,72,256]{2,1,0:T(8,128)(2,1)}), bf16[32,72,256]{2,1,0:T(8,128)(2,1)}, u32[]{:S(2)}, u32[]{:S(2)}) %all-to-all-start) | async-done | bytes 1179680 | tf_op jit(solution)/shard_map/all_to_all | solution.py:617
  42.9 6.7 %shard_map.174 = (bf16[128,256]{1,0:T(8,128)(2,1)}, f32[128,256]{1,0:T(8,128)}, f32[16,72,256]{2,1,0:T(8,128)}, bf16[16,72,256]{2,1,0:T(8,128)(2,1)}) custom-call(s32[1]{0:T(128)} %bitcast.8.refs_0_, s32[4,64]{1,0:T(4,128)} %bitcast.16, s32[4,64]{1,0:T(4,128)} %bitcast.19, bf16[32,32,256]{2,1,0:T(8,128)(2,1)} %bitcast.23, bf16[32,32,256]{2,1,0:T(8,128)(2,1)} %bitcast.25, ...), custom_call_target="tpu_custom_call" | custom-call | tf_op jit(solution)/shard_map/pallas_call | solution.py:74
  49.7 0.5 collective-permute-start.1
  50.2 1.8 %collective-permute-done.1 = bf16[16,72,256]{2,1,0:T(8,128)(2,1)S(1)} collective-permute-done((bf16[16,72,256]{2,1,0:T(8,128)(2,1)}, bf16[16,72,256]{2,1,0:T(8,128)(2,1)S(1)}, u32[]{:S(2)}, u32[]{:S(2)}) %collective-permute-start.1) | collective-permute-done | bytes 589856 | tf_op jit(solution)/shard_map/ppermute | solution.py:628
  52.0 2.2 %add_convert_fusion = bf16[16,72,256]{2,1,0:T(8,128)(2,1)} fusion(f32[16,72,256]{2,1,0:T(8,128)} %get-tuple-element.29, bf16[16,72,256]{2,1,0:T(8,128)(2,1)S(1)} %collective-permute-done.1), kind=kLoop, calls=%fused_computation.1 | loop fusion | flops 884736 | bytes 2359296 | tf_op jit(solution)/shard_map/convert_element_type | solution.py:629
  54.2 3.6 %all-to-all-start.1 = ((bf16[16,72,256]{2,1,0:T(8,128)(2,1)}), bf16[16,72,256]{2,1,0:T(8,128)(2,1)S(1)}, u32[]{:S(2)}, u32[]{:S(2)}) async-start(bf16[16,72,256]{2,1,0:T(8,128)(2,1)} %add_convert_fusion), calls=%async_computation.1 | async-start | bytes 1179648 | tf_op jit(solution)/shard_map/all_to_all | solution.py:624
  57.8 1.8 %shard_map.176 = (f32[8,32,256]{2,1,0:T(8,128)}, bf16[136,256]{1,0:T(8,128)(2,1)}) custom-call(f32[128,256]{1,0:T(8,128)} %get-tuple-element.27.refs_0_, f32[9,256]{1,0:T(8,128)} %refs_1_.1), custom_call_target="tpu_custom_call" | custom-call | tf_op jit(solution)/shard_map/pallas_call | solution.py:74
  59.6 6.1 %collective-permute-start.6 = (bf16[136,256]{1,0:T(8,128)(2,1)}, bf16[136,256]{1,0:T(8,128)(2,1)S(1)}, u32[]{:S(2)}, u32[]{:S(2)}) collective-permute-start(bf16[136,256]{1,0:T(8,128)(2,1)} %get-tuple-element.31.refs_2_), channel_id=1, source_target_pairs={{0,8},{4,12},{8,0},{12,4},{16,24},{20,28},{24,16},{28,20},{32,40},... | collective-permute-start | bytes 208904 | tf_op jit(solution)/shard_map/ppermute | solution.py:669
  65.6 2.4 %collective-permute-done.6.refs_3_ = bf16[136,256]{1,0:T(8,128)(2,1)S(1)} collective-permute-done((bf16[136,256]{1,0:T(8,128)(2,1)}, bf16[136,256]{1,0:T(8,128)(2,1)S(1)}, u32[]{:S(2)}, u32[]{:S(2)}) %collective-permute-start.6) | collective-permute-done | bytes 69664 | tf_op jit(solution)/shard_map/ppermute | solution.py:669
  68.0 0.0 copy-start.7
  68.0 0.6 copy-done.7
  68.7 2.4 %shard_map.177 = bf16[32,72,256]{2,1,0:T(8,128)(2,1)} custom-call(s32[1]{0:T(128)} %bitcast.8.refs_0_, s32[4,64]{1,0:T(4,128)} %bitcast.17, bf16[136,256]{1,0:T(8,128)(2,1)} %get-tuple-element.31.refs_2_, bf16[136,256]{1,0:T(8,128)(2,1)} %copy-done.7), custom_call_target="tpu_custom_call" | custom-call | tf_op jit(solution)/shard_map/pallas_call | solution.py:74
  71.1 0.0 all-to-all-done.1
  71.1 8.9 %all-to-all-start.2 = ((bf16[32,72,256]{2,1,0:T(8,128)(2,1)}), bf16[32,72,256]{2,1,0:T(8,128)(2,1)S(1)}, u32[]{:S(2)}, u32[]{:S(2)}) async-start(bf16[32,72,256]{2,1,0:T(8,128)(2,1)} %shard_map.177), calls=%async_computation.2 | async-start | bytes 2359296 | tf_op jit(solution)/shard_map/all_to_all | solution.py:617
  79.9 0.1 convert_reduce_fusion
  80.0 6.1 %collective-permute-start.2 = (bf16[72,256]{1,0:T(8,128)(2,1)S(1)}, bf16[72,256]{1,0:T(8,128)(2,1)S(1)}, u32[]{:S(2)}, u32[]{:S(2)}) collective-permute-start(bf16[72,256]{1,0:T(8,128)(2,1)S(1)} %convert_reduce_fusion), channel_id=1, source_target_pairs={{0,8},{4,12},{8,0},{12,4},{16,24},{20,28},{24,16},{28,20},{32,40},... | collective-permute-start | bytes 110600 | tf_op jit(solution)/shard_map/ppermute | solution.py:634
  86.1 1.5 %collective-permute-done.2 = bf16[72,256]{1,0:T(8,128)(2,1)S(1)} collective-permute-done((bf16[72,256]{1,0:T(8,128)(2,1)S(1)}, bf16[72,256]{1,0:T(8,128)(2,1)S(1)}, u32[]{:S(2)}, u32[]{:S(2)}) %collective-permute-start.2) | collective-permute-done | bytes 36896 | tf_op jit(solution)/shard_map/ppermute | solution.py:634
  87.6 0.9 collective-permute-start.5
  88.5 1.3 %collective-permute-start.4 = (bf16[72,256]{1,0:T(8,128)(2,1)S(1)}, bf16[72,256]{1,0:T(8,128)(2,1)S(1)}, u32[]{:S(2)}, u32[]{:S(2)}) collective-permute-start(bf16[72,256]{1,0:T(8,128)(2,1)S(1)} %add_convert_fusion.2), channel_id=1, source_target_pairs={{0,1},{1,2},{2,3},{3,0},{4,5},{5,6},{6,7},{7,4},{8,9},{9,10},{10,1... | collective-permute-start | bytes 110600 | tf_op jit(solution)/shard_map/ppermute | solution.py:638
  89.8 2.3 %collective-permute-start.3 = (bf16[72,256]{1,0:T(8,128)(2,1)S(1)}, bf16[72,256]{1,0:T(8,128)(2,1)S(1)}, u32[]{:S(2)}, u32[]{:S(2)}) collective-permute-start(bf16[72,256]{1,0:T(8,128)(2,1)S(1)} %add_convert_fusion.2), channel_id=1, source_target_pairs={{0,2},{1,3},{2,0},{3,1},{4,6},{5,7},{6,4},{7,5},{8,10},{9,11},{10,... | collective-permute-start | bytes 110600 | tf_op jit(solution)/shard_map/ppermute | solution.py:638
  92.1 0.0 collective-permute-done.5
  92.1 1.7 %collective-permute-done.4 = bf16[72,256]{1,0:T(8,128)(2,1)S(1)} collective-permute-done((bf16[72,256]{1,0:T(8,128)(2,1)S(1)}, bf16[72,256]{1,0:T(8,128)(2,1)S(1)}, u32[]{:S(2)}, u32[]{:S(2)}) %collective-permute-start.4) | collective-permute-done | bytes 36896 | tf_op jit(solution)/shard_map/ppermute | solution.py:638
  93.9 0.6 collective-permute-done.3
  94.5 4.0 %all-to-all-done.2.refs_5_ = bf16[32,72,256]{2,1,0:T(8,128)(2,1)S(1)} async-done(((bf16[32,72,256]{2,1,0:T(8,128)(2,1)}), bf16[32,72,256]{2,1,0:T(8,128)(2,1)S(1)}, u32[]{:S(2)}, u32[]{:S(2)}) %all-to-all-start.2) | async-done | bytes 1179680 | tf_op jit(solution)/shard_map/all_to_all | solution.py:617
  98.5 1.0 copy-done
  99.6 0.0 copy-start.3
  99.6 0.0 copy-start.4
  99.6 0.0 copy-start.5
  99.6 13.8 %all_to_all.20.refs_1_ = bf16[16,72,256]{2,1,0:T(8,128)(2,1)S(1)} all-to-all(bf16[16,72,256]{2,1,0:T(8,128)(2,1)S(1)} %broadcast_in_dim.14), channel_id=1, replica_groups={{0,64,128,192,16,80,144,208,32,96,160,224,48,112,176,240},{4,68,132,196..., dimensions={0} | all-to-all | bytes 1179648 | tf_op jit(solution)/shard_map/all_to_all | solution.py:624
  113.4 2.6 %collective-permute-start.7 = (bf16[16,72,256]{2,1,0:T(8,128)(2,1)S(1)}, bf16[16,72,256]{2,1,0:T(8,128)(2,1)}, u32[]{:S(2)}, u32[]{:S(2)}) collective-permute-start(bf16[16,72,256]{2,1,0:T(8,128)(2,1)S(1)} %all_to_all.20.refs_1_), channel_id=1, source_target_pairs={{0,4},{4,0},{8,12},{12,8},{16,20},{20,16},{24,28},{28,24},{32,36},... | collective-permute-start | bytes 1769480 | tf_op jit(solution)/shard_map/ppermute | solution.py:643
  116.0 2.0 %shard_map.175 = bf16[32,32,256]{2,1,0:T(8,128)(2,1)} custom-call(bf16[32,32,256]{2,1,0:T(8,128)(2,1)} %bitcast.27, bf16[128,256]{1,0:T(8,128)(2,1)} %get-tuple-element.25.refs_1_), custom_call_target="tpu_custom_call" | custom-call | tf_op jit(solution)/shard_map/pallas_call | solution.py:74
  118.0 0.0 copy-done.3
  118.0 0.0 copy-done.4
  118.0 0.0 copy-done.5
  118.0 0.0 copy-start.1
  118.0 1.3 copy-done.1
  119.3 1.2 copy-done.2
  120.5 1.8 %shard_map.178 = bf16[32,32,256]{2,1,0:T(8,128)(2,1)} custom-call(s32[1]{0:T(128)} %bitcast.8.refs_0_, s32[4,64]{1,0:T(4,128)S(1)} %bitcast.18, s32[4,64]{1,0:T(4,128)S(1)} %bitcast.20, f32[32,32,256]{2,1,0:T(8,128)S(1)} %copy-done.2, f32[8,32,256]{2,1,0:T(8,128)S(1)} %copy-done.3, bf16[32,72,256]{2,1,0:T(8,128)(2,1)S(1)} %copy-done.1), custom_call_target="tpu_custom_call" | custom-call | tf_op jit(solution)/shard_map/pallas_call | solution.py:74
  122.3 0.0 collective-permute-done.7.refs_2_
  122.3 3.9 %shard_map.179 = (f32[9,256]{1,0:T(8,128)}, f32[4,256]{1,0:T(4,128)}, f32[256,1024]{1,0:T(8,128)}, f32[1,1024]{1,0:T(1,128)}, f32[1024,256]{1,0:T(8,128)}) custom-call(s32[1]{0:T(128)} %bitcast.8.refs_0_, bf16[16,72,256]{2,1,0:T(8,128)(2,1)S(1)} %all_to_all.20.refs_1_, bf16[16,72,256]{2,1,0:T(8,128)(2,1)} %collective-permute-done.7.refs_2_), custom_call_target="tpu_custom_call" | custom-call | tf_op jit(solution)/shard_map/pallas_call | solution.py:74
  (5 shorter events, 0.1 us)
Async XLA Ops:
  2.5 9.8 %collective-permute-start = (bf16[136,256]{1,0:T(8,128)(2,1)}, bf16[136,256]{1,0:T(8,128)(2,1)S(1)}, u32[]{:S(2)}, u32[]{:S(2)}) collective-permute-start(bf16[136,256]{1,0:T(8,128)(2,1)} %shard_map.172.refs_2_), channel_id=1, source_target_pairs={{0,8},{4,12},{8,0},{12,4},{16,24},{20,28},{24,16},{28,20},{32,40},... | collective-permute-start | bytes 208904 | tf_op jit(solution)/shard_map/ppermute | solution.py:669
  12.3 0.6 copy-start.6
  15.3 27.6 %all-to-all-start = ((bf16[32,72,256]{2,1,0:T(8,128)(2,1)}), bf16[32,72,256]{2,1,0:T(8,128)(2,1)}, u32[]{:S(2)}, u32[]{:S(2)}) async-start(bf16[32,72,256]{2,1,0:T(8,128)(2,1)} %shard_map.173), calls=%async_computation | async-start | bytes 2359296 | tf_op jit(solution)/shard_map/all_to_all | solution.py:617
  49.7 2.3 %collective-permute-start.1 = (bf16[16,72,256]{2,1,0:T(8,128)(2,1)}, bf16[16,72,256]{2,1,0:T(8,128)(2,1)S(1)}, u32[]{:S(2)}, u32[]{:S(2)}) collective-permute-start(bf16[16,72,256]{2,1,0:T(8,128)(2,1)} %get-tuple-element.30), channel_id=1, source_target_pairs={{0,4},{4,0},{8,12},{12,8},{16,20},{20,16},{24,28},{28,24},{32,36},... | collective-permute-start | bytes 1769480 | tf_op jit(solution)/shard_map/ppermute | solution.py:628
  54.2 16.9 %all-to-all-start.1 = ((bf16[16,72,256]{2,1,0:T(8,128)(2,1)}), bf16[16,72,256]{2,1,0:T(8,128)(2,1)S(1)}, u32[]{:S(2)}, u32[]{:S(2)}) async-start(bf16[16,72,256]{2,1,0:T(8,128)(2,1)} %add_convert_fusion), calls=%async_computation.1 | async-start | bytes 1179648 | tf_op jit(solution)/shard_map/all_to_all | solution.py:624
  59.6 8.5 %collective-permute-start.6 = (bf16[136,256]{1,0:T(8,128)(2,1)}, bf16[136,256]{1,0:T(8,128)(2,1)S(1)}, u32[]{:S(2)}, u32[]{:S(2)}) collective-permute-start(bf16[136,256]{1,0:T(8,128)(2,1)} %get-tuple-element.31.refs_2_), channel_id=1, source_target_pairs={{0,8},{4,12},{8,0},{12,4},{16,24},{20,28},{24,16},{28,20},{32,40},... | collective-permute-start | bytes 208904 | tf_op jit(solution)/shard_map/ppermute | solution.py:669
  68.0 0.6 copy-start.7
  71.1 27.4 %all-to-all-start.2 = ((bf16[32,72,256]{2,1,0:T(8,128)(2,1)}), bf16[32,72,256]{2,1,0:T(8,128)(2,1)S(1)}, u32[]{:S(2)}, u32[]{:S(2)}) async-start(bf16[32,72,256]{2,1,0:T(8,128)(2,1)} %shard_map.177), calls=%async_computation.2 | async-start | bytes 2359296 | tf_op jit(solution)/shard_map/all_to_all | solution.py:617
  80.0 7.5 %collective-permute-start.2 = (bf16[72,256]{1,0:T(8,128)(2,1)S(1)}, bf16[72,256]{1,0:T(8,128)(2,1)S(1)}, u32[]{:S(2)}, u32[]{:S(2)}) collective-permute-start(bf16[72,256]{1,0:T(8,128)(2,1)S(1)} %convert_reduce_fusion), channel_id=1, source_target_pairs={{0,8},{4,12},{8,0},{12,4},{16,24},{20,28},{24,16},{28,20},{32,40},... | collective-permute-start | bytes 110600 | tf_op jit(solution)/shard_map/ppermute | solution.py:634
  87.6 4.6 %collective-permute-start.5 = (bf16[72,256]{1,0:T(8,128)(2,1)S(1)}, bf16[72,256]{1,0:T(8,128)(2,1)S(1)}, u32[]{:S(2)}, u32[]{:S(2)}) collective-permute-start(bf16[72,256]{1,0:T(8,128)(2,1)S(1)} %add_convert_fusion.2), channel_id=1, source_target_pairs={{0,3},{1,0},{2,1},{3,2},{4,7},{5,4},{6,5},{7,6},{8,11},{9,8},{10,9... | collective-permute-start | bytes 110600 | tf_op jit(solution)/shard_map/ppermute | solution.py:638
  88.5 5.4 %collective-permute-start.4 = (bf16[72,256]{1,0:T(8,128)(2,1)S(1)}, bf16[72,256]{1,0:T(8,128)(2,1)S(1)}, u32[]{:S(2)}, u32[]{:S(2)}) collective-permute-start(bf16[72,256]{1,0:T(8,128)(2,1)S(1)} %add_convert_fusion.2), channel_id=1, source_target_pairs={{0,1},{1,2},{2,3},{3,0},{4,5},{5,6},{6,7},{7,4},{8,9},{9,10},{10,1... | collective-permute-start | bytes 110600 | tf_op jit(solution)/shard_map/ppermute | solution.py:638
  89.8 4.7 %collective-permute-start.3 = (bf16[72,256]{1,0:T(8,128)(2,1)S(1)}, bf16[72,256]{1,0:T(8,128)(2,1)S(1)}, u32[]{:S(2)}, u32[]{:S(2)}) collective-permute-start(bf16[72,256]{1,0:T(8,128)(2,1)S(1)} %add_convert_fusion.2), channel_id=1, source_target_pairs={{0,2},{1,3},{2,0},{3,1},{4,6},{5,7},{6,4},{7,5},{8,10},{9,11},{10,... | collective-permute-start | bytes 110600 | tf_op jit(solution)/shard_map/ppermute | solution.py:638
  98.5 1.0 copy-start
  99.6 18.5 %copy-start.3 = (f32[8,32,256]{2,1,0:T(8,128)S(1)}, f32[8,32,256]{2,1,0:T(8,128)}, u32[]{:S(2)}) copy-start(f32[8,32,256]{2,1,0:T(8,128)} %get-tuple-element.28.refs_4_) | copy-start | bytes 786436
  99.6 18.5 %copy-start.4 = (s32[64,4]{0,1:T(4,128)S(1)}, s32[64,4]{0,1:T(4,128)}, u32[]{:S(2)}) copy-start(s32[64,4]{0,1:T(4,128)} %param.22) | copy-start | bytes 3076
  99.6 18.5 %copy-start.5 = (s32[64,4]{0,1:T(4,128)S(1)}, s32[64,4]{0,1:T(4,128)}, u32[]{:S(2)}) copy-start(s32[64,4]{0,1:T(4,128)} %param.23) | copy-start | bytes 3076
  113.4 8.9 %collective-permute-start.7 = (bf16[16,72,256]{2,1,0:T(8,128)(2,1)S(1)}, bf16[16,72,256]{2,1,0:T(8,128)(2,1)}, u32[]{:S(2)}, u32[]{:S(2)}) collective-permute-start(bf16[16,72,256]{2,1,0:T(8,128)(2,1)S(1)} %all_to_all.20.refs_1_), channel_id=1, source_target_pairs={{0,4},{4,0},{8,12},{12,8},{16,20},{20,16},{24,28},{28,24},{32,36},... | collective-permute-start | bytes 1769480 | tf_op jit(solution)/shard_map/ppermute | solution.py:643
  118.0 1.3 %copy-start.1 = (bf16[32,72,256]{2,1,0:T(8,128)(2,1)S(1)}, bf16[32,72,256]{2,1,0:T(8,128)(2,1)}, u32[]{:S(2)}) copy-start(bf16[32,72,256]{2,1,0:T(8,128)(2,1)} %copy-done) | copy-start | bytes 3538948
  119.3 1.2 copy-start.2

commit v2 on v1

--- a/solution.py
+++ b/solution.py
@@ -211,6 +211,7 @@
     blocks_ref,
     base_ref,
     grad_ref,
+    edge_ref,
     pad_ref,
     xhat_ref,
     istd_ref,
@@ -226,6 +227,15 @@
     pad_ref[1, pl.ds(1, S)] = center
     pad_ref[0, pl.ds(1, S)] = pltpu.roll(center, 1, 1)
     pad_ref[2, pl.ds(1, S)] = pltpu.roll(center, S - 1, 1)
+
+    last = S - 1
+    for n, i in enumerate((0, 1, last - 1, last)):
+        edge_ref[n] = pad_ref[1, i + 1].astype(BF)
+        edge_ref[4 + n] = pad_ref[1, pl.ds(1, S), i, :].astype(BF)
+    dconv_ref[...] = cot_ref[...].astype(F32).reshape(S, S, C)
+    for n, i in enumerate((0, last)):
+        edge_ref[8 + n] = dconv_ref[i].astype(BF)
+        edge_ref[10 + n] = dconv_ref[:, i, :].astype(BF)
 
     bias = bias_ref[...]
     gain = gain_ref[...]
@@ -331,8 +341,7 @@
     pos_ref,
     seam_ref,
     corner_ref,
-    field_ref,
-    cot_ref,
+    edge_ref,
     recv_ref,
     kern_ref,
     bias_ref,
@@ -347,16 +356,15 @@
     dconv_ref,
     own_ref,
     send_ref,
-    wide_ref,
 ):
     pos = pos_ref[0]
     core = pos % 2
     strips, cells = take_slots(recv_ref, pos, seam_ref, corner_ref)
     top, bottom, left, right = strips
     last = S - 1
-    wide_ref[...] = field_ref[...].astype(F32)
-    at_row = lambda i: wide_ref[i]
-    at_col = lambda j: wide_ref[:, j, :]
+    order = {0: 0, 1: 1, last - 1: 2, last: 3}
+    at_row = lambda i: edge_ref[order[i]].astype(F32)
+    at_col = lambda j: edge_ref[4 + order[j]].astype(F32)
     spot = lambda line, i: line[i : i + 1]
     place = lax.broadcasted_iota(jnp.int32, (S, C), 0)
     flat = lambda k: kern_ref[k : k + 1, :]
@@ -404,17 +412,16 @@
                 acc = acc + window * flat(k)
         rows.append(acc)
     field_rows = jnp.concatenate([lines[1] for lines, _, _ in bands], axis=0)
-    wide_ref[...] = cot_ref[...].astype(F32)
     once = (place > 0) & (place < last)
     cot_rows = jnp.concatenate(
-        [at_row(0), at_row(last)]
-        + [jnp.where(once, at_col(0), 0.0), jnp.where(once, at_col(last), 0.0)],
+        [edge_ref[8].astype(F32), edge_ref[9].astype(F32)]
+        + [jnp.where(once, edge_ref[n].astype(F32), 0.0) for n in (10, 11)],
         axis=0,
     ).astype(BF)
 
     gain = gain_ref[...]
-    waits[11]()
-    waits[13]()
+    waits[10]()
+    waits[12]()
     xhat, istd = norm_rows(jnp.concatenate(rows, axis=0))
     normed = (xhat * gain + shift_ref[...]).astype(BF)
     kept = []
@@ -434,7 +441,7 @@
 
     dconv_ref[...] = dconv
 
-    waits[14]()
+    waits[13]()
 
     def put_rows(first, value):
         mine = core == first // 16
@@ -638,8 +645,9 @@
     got = [mine] + [lax.ppermute(mine, "batch", turn(d)) for d in (1, 2, 3)]
     got = [g.astype(F32) for g in got]
     piece = (got[0] + got[2]) + (got[1] + got[3])
-    piece, back = lax.optimization_barrier((piece.astype(BF), back))
-    full = plane(jnp.broadcast_to(piece[None], (16, CHUNK, C)))
+    spread = jnp.broadcast_to(piece.astype(BF)[None], (16, CHUNK, C))
+    spread, back = lax.optimization_barrier((spread, back))
+    full = plane(spread)
     return full, lax.ppermute(full, "space", moves("c", 1)), back
 
 
@@ -690,13 +698,14 @@
         row(b_in),
         (w_out, "vmem", 1),
     ]
-    part, base, grads = staged_call(
+    part, base, grads, border_lines = staged_call(
         inside_kernel,
         [(field, "vmem", 0), (cot.reshape(cells, C), "vmem", 0)] + weights,
         [
             (sds((cells, C), BF), True),
             (sds((S, S, C), F32), True),
             (sds((32, CHUNK, C), F32), True),
+            (sds((12, S, C), BF), True),
         ],
         [
             pltpu.VMEM((3, S + 2, S, C), F32),
@@ -717,7 +726,7 @@
     border_rows, dconv, own, send = staged_call(
         border_kernel,
         where
-        + [(field, "vmem", 0), (cot, "vmem", 0), (halo, "vmem", 0)]
+        + [(border_lines, "vmem", 0), (halo, "vmem", 0)]
         + weights
         + [(grads, "vmem", 1)],
         [
@@ -726,7 +735,7 @@
             (sds((16, CHUNK, C), F32), True),
             (sds((16, CHUNK, C), BF), True),
         ],
-        [wide],
+        [],
         63,
     )
     lines, rim = staged_call(

time: 127 us -> 127 us (level)
  no operation moved by 1% of the time
where the time goes in v2:
time: 127 us; the launch traced here: 126 us
  starting transfers between devices  49.1 us (39%)
  Pallas kernels  37.5 us (30%)
  waiting for transfers between devices  17.6 us (14%)
  blocking collectives  13.8 us (11%)
  local copies, waits for them, and re-layouts  4.83 us (4%)
  other arithmetic  2.33 us (2%)
    pallas_call x9, Pallas kernels, staged_call(): pl.pallas_call(body, out_shape=tuple((o for o, _ in outs)), in_specs=[VME...  37.5 us
    all_to_all x2, starting transfers between devices, exchange(): lax.all_to_all(slots, 'space', 0, 0, axis_index_groups=halves, tiled=True)  17.9 us
    ppermute x2, starting transfers between devices, to_slots(): other = lax.ppermute(mine, 'space', moves('h', 1))  13.9 us
    all_to_all x1, blocking collectives, plane(): lax.all_to_all(slots, 'space', 0, 0, axis_index_groups=planes, tiled=True)  13.8 us
    all_to_all x2, waiting for transfers between devices, exchange(): lax.all_to_all(slots, 'space', 0, 0, axis_index_groups=halves, tiled=True)  7.59 us
    ppermute x1, starting transfers between devices, sum_over_devices(): other = lax.ppermute(mine, 'space', moves('h', 1))  6.06 us
    unnamed x16, local copies, waits for them, and re-layouts  4.79 us
    ppermute x3, starting transfers between devices, sum_over_devices(): got = [mine] + [lax.ppermute(mine, 'batch', turn(d)) for d in (1, 2, 3)]  4.57 us
  transfers between devices with their start and end apart: 11, of which 8 were waited for; matrix products, arithmetic and copies ran while one was open for 0% of the time, Pallas kernels for 18%

profile of v2, /device:TPU:1, one launch (start us, length us, event | category | flops | bytes accessed | tf_op | source)
XLA Modules:
  0.0 126.1 jit_solution(5505244809698093180)
XLA Ops:
  0.6 1.8 %shard_map.172.refs_2_ = bf16[136,256]{1,0:T(8,128)(2,1)} custom-call(bf16[32,32,256]{2,1,0:T(8,128)(2,1)} %bitcast.21), custom_call_target="tpu_custom_call" | custom-call | tf_op jit(solution)/shard_map/pallas_call | solution.py:74
  2.5 7.8 %collective-permute-start = (bf16[136,256]{1,0:T(8,128)(2,1)}, bf16[136,256]{1,0:T(8,128)(2,1)S(1)}, u32[]{:S(2)}, u32[]{:S(2)}) collective-permute-start(bf16[136,256]{1,0:T(8,128)(2,1)} %shard_map.172.refs_2_), channel_id=1, source_target_pairs={{0,8},{4,12},{8,0},{12,4},{16,24},{20,28},{24,16},{28,20},{32,40},... | collective-permute-start | bytes 208904 | tf_op jit(solution)/shard_map/ppermute | solution.py:677
  10.3 2.0 %collective-permute-done.refs_3_ = bf16[136,256]{1,0:T(8,128)(2,1)S(1)} collective-permute-done((bf16[136,256]{1,0:T(8,128)(2,1)}, bf16[136,256]{1,0:T(8,128)(2,1)S(1)}, u32[]{:S(2)}, u32[]{:S(2)}) %collective-permute-start) | collective-permute-done | bytes 69664 | tf_op jit(solution)/shard_map/ppermute | solution.py:677
  12.3 0.0 copy-start.6
  12.3 0.6 copy-done.6
  12.9 2.4 %shard_map.173 = bf16[32,72,256]{2,1,0:T(8,128)(2,1)} custom-call(s32[1]{0:T(128)} %bitcast.8.refs_0_, s32[4,64]{1,0:T(4,128)} %bitcast.14, bf16[136,256]{1,0:T(8,128)(2,1)} %shard_map.172.refs_2_, bf16[136,256]{1,0:T(8,128)(2,1)} %copy-done.6), custom_call_target="tpu_custom_call" | custom-call | tf_op jit(solution)/shard_map/pallas_call | solution.py:74
  15.3 9.0 %all-to-all-start = ((bf16[32,72,256]{2,1,0:T(8,128)(2,1)}), bf16[32,72,256]{2,1,0:T(8,128)(2,1)}, u32[]{:S(2)}, u32[]{:S(2)}) async-start(bf16[32,72,256]{2,1,0:T(8,128)(2,1)} %shard_map.173), calls=%async_computation | async-start | bytes 2359296 | tf_op jit(solution)/shard_map/all_to_all | solution.py:624
  24.3 15.0 %shard_map.171 = (bf16[1024,256]{1,0:T(8,128)(2,1)}, f32[32,32,256]{2,1,0:T(8,128)}, f32[32,72,256]{2,1,0:T(8,128)}, bf16[12,32,256]{2,1,0:T(8,128)(2,1)}) custom-call(bf16[32,32,256]{2,1,0:T(8,128)(2,1)} %bitcast.22, bf16[1024,256]{1,0:T(8,128)(2,1)} %bitcast.35, f32[9,256]{1,0:T(8,128)} %refs_1_.1, f32[1,256]{1,0:T(1,128)} %bitcast.27, f32[1,256]{1,0:T(1,128)} %bitcast.29, ...), custom_call_target="tpu_custom_call" | custom-call | flops 3221225472 | bytes 8388608 | tf_op jit(solution)/shard_map/pallas_call | solution.py:74
  39.3 3.6 %all-to-all-done.refs_4_ = bf16[32,72,256]{2,1,0:T(8,128)(2,1)} async-done(((bf16[32,72,256]{2,1,0:T(8,128)(2,1)}), bf16[32,72,256]{2,1,0:T(8,128)(2,1)}, u32[]{:S(2)}, u32[]{:S(2)}) %all-to-all-start) | async-done | bytes 1179680 | tf_op jit(solution)/shard_map/all_to_all | solution.py:624
  42.9 6.5 %shard_map.174 = (bf16[128,256]{1,0:T(8,128)(2,1)}, f32[128,256]{1,0:T(8,128)}, f32[16,72,256]{2,1,0:T(8,128)}, bf16[16,72,256]{2,1,0:T(8,128)(2,1)}) custom-call(s32[1]{0:T(128)} %bitcast.8.refs_0_, s32[4,64]{1,0:T(4,128)} %bitcast.15, s32[4,64]{1,0:T(4,128)} %bitcast.18, bf16[12,32,256]{2,1,0:T(8,128)(2,1)} %get-tuple-element.25.refs_3_, ...), custom_call_target="tpu_custom_call" | custom-call | tf_op jit(solution)/shard_map/pallas_call | solution.py:74
  49.4 0.5 collective-permute-start.1
  49.9 1.8 %collective-permute-done.1 = bf16[16,72,256]{2,1,0:T(8,128)(2,1)S(1)} collective-permute-done((bf16[16,72,256]{2,1,0:T(8,128)(2,1)}, bf16[16,72,256]{2,1,0:T(8,128)(2,1)S(1)}, u32[]{:S(2)}, u32[]{:S(2)}) %collective-permute-start.1) | collective-permute-done | bytes 589856 | tf_op jit(solution)/shard_map/ppermute | solution.py:635
  51.7 2.2 %add_convert_fusion = bf16[16,72,256]{2,1,0:T(8,128)(2,1)} fusion(f32[16,72,256]{2,1,0:T(8,128)} %get-tuple-element.31, bf16[16,72,256]{2,1,0:T(8,128)(2,1)S(1)} %collective-permute-done.1), kind=kLoop, calls=%fused_computation.1 | loop fusion | flops 884736 | bytes 2359296 | tf_op jit(solution)/shard_map/convert_element_type | solution.py:636
  53.9 3.6 %all-to-all-start.1 = ((bf16[16,72,256]{2,1,0:T(8,128)(2,1)}), bf16[16,72,256]{2,1,0:T(8,128)(2,1)S(1)}, u32[]{:S(2)}, u32[]{:S(2)}) async-start(bf16[16,72,256]{2,1,0:T(8,128)(2,1)} %add_convert_fusion), calls=%async_computation.1 | async-start | bytes 1179648 | tf_op jit(solution)/shard_map/all_to_all | solution.py:631
  57.5 1.7 %shard_map.176 = (f32[8,32,256]{2,1,0:T(8,128)}, bf16[136,256]{1,0:T(8,128)(2,1)}) custom-call(f32[128,256]{1,0:T(8,128)} %get-tuple-element.29.refs_0_, f32[9,256]{1,0:T(8,128)} %refs_1_.1), custom_call_target="tpu_custom_call" | custom-call | tf_op jit(solution)/shard_map/pallas_call | solution.py:74
  59.3 6.1 %collective-permute-start.6 = (bf16[136,256]{1,0:T(8,128)(2,1)}, bf16[136,256]{1,0:T(8,128)(2,1)S(1)}, u32[]{:S(2)}, u32[]{:S(2)}) collective-permute-start(bf16[136,256]{1,0:T(8,128)(2,1)} %get-tuple-element.33.refs_2_), channel_id=1, source_target_pairs={{0,8},{4,12},{8,0},{12,4},{16,24},{20,28},{24,16},{28,20},{32,40},... | collective-permute-start | bytes 208904 | tf_op jit(solution)/shard_map/ppermute | solution.py:677
  65.3 2.4 %collective-permute-done.6.refs_3_ = bf16[136,256]{1,0:T(8,128)(2,1)S(1)} collective-permute-done((bf16[136,256]{1,0:T(8,128)(2,1)}, bf16[136,256]{1,0:T(8,128)(2,1)S(1)}, u32[]{:S(2)}, u32[]{:S(2)}) %collective-permute-start.6) | collective-permute-done | bytes 69664 | tf_op jit(solution)/shard_map/ppermute | solution.py:677
  67.7 0.0 copy-start.7
  67.7 0.6 copy-done.7
  68.4 2.4 %shard_map.177 = bf16[32,72,256]{2,1,0:T(8,128)(2,1)} custom-call(s32[1]{0:T(128)} %bitcast.8.refs_0_, s32[4,64]{1,0:T(4,128)} %bitcast.16, bf16[136,256]{1,0:T(8,128)(2,1)} %get-tuple-element.33.refs_2_, bf16[136,256]{1,0:T(8,128)(2,1)} %copy-done.7), custom_call_target="tpu_custom_call" | custom-call | tf_op jit(solution)/shard_map/pallas_call | solution.py:74
  70.8 0.0 all-to-all-done.1
  70.8 8.9 %all-to-all-start.2 = ((bf16[32,72,256]{2,1,0:T(8,128)(2,1)}), bf16[32,72,256]{2,1,0:T(8,128)(2,1)S(1)}, u32[]{:S(2)}, u32[]{:S(2)}) async-start(bf16[32,72,256]{2,1,0:T(8,128)(2,1)} %shard_map.177), calls=%async_computation.2 | async-start | bytes 2359296 | tf_op jit(solution)/shard_map/all_to_all | solution.py:624
  79.6 0.1 convert_reduce_fusion
  79.7 6.1 %collective-permute-start.2 = (bf16[72,256]{1,0:T(8,128)(2,1)S(1)}, bf16[72,256]{1,0:T(8,128)(2,1)S(1)}, u32[]{:S(2)}, u32[]{:S(2)}) collective-permute-start(bf16[72,256]{1,0:T(8,128)(2,1)S(1)} %convert_reduce_fusion), channel_id=1, source_target_pairs={{0,8},{4,12},{8,0},{12,4},{16,24},{20,28},{24,16},{28,20},{32,40},... | collective-permute-start | bytes 110600 | tf_op jit(solution)/shard_map/ppermute | solution.py:641
  85.8 1.5 %collective-permute-done.2 = bf16[72,256]{1,0:T(8,128)(2,1)S(1)} collective-permute-done((bf16[72,256]{1,0:T(8,128)(2,1)S(1)}, bf16[72,256]{1,0:T(8,128)(2,1)S(1)}, u32[]{:S(2)}, u32[]{:S(2)}) %collective-permute-start.2) | collective-permute-done | bytes 36896 | tf_op jit(solution)/shard_map/ppermute | solution.py:641
  87.3 0.9 collective-permute-start.5
  88.2 1.5 %collective-permute-start.4 = (bf16[72,256]{1,0:T(8,128)(2,1)S(1)}, bf16[72,256]{1,0:T(8,128)(2,1)S(1)}, u32[]{:S(2)}, u32[]{:S(2)}) collective-permute-start(bf16[72,256]{1,0:T(8,128)(2,1)S(1)} %add_convert_fusion.2), channel_id=1, source_target_pairs={{0,1},{1,2},{2,3},{3,0},{4,5},{5,6},{6,7},{7,4},{8,9},{9,10},{10,1... | collective-permute-start | bytes 110600 | tf_op jit(solution)/shard_map/ppermute | solution.py:645
  89.7 2.2 %collective-permute-start.3 = (bf16[72,256]{1,0:T(8,128)(2,1)S(1)}, bf16[72,256]{1,0:T(8,128)(2,1)S(1)}, u32[]{:S(2)}, u32[]{:S(2)}) collective-permute-start(bf16[72,256]{1,0:T(8,128)(2,1)S(1)} %add_convert_fusion.2), channel_id=1, source_target_pairs={{0,2},{1,3},{2,0},{3,1},{4,6},{5,7},{6,4},{7,5},{8,10},{9,11},{10,... | collective-permute-start | bytes 110600 | tf_op jit(solution)/shard_map/ppermute | solution.py:645
  91.8 0.0 collective-permute-done.5
  91.8 1.7 %collective-permute-done.4 = bf16[72,256]{1,0:T(8,128)(2,1)S(1)} collective-permute-done((bf16[72,256]{1,0:T(8,128)(2,1)S(1)}, bf16[72,256]{1,0:T(8,128)(2,1)S(1)}, u32[]{:S(2)}, u32[]{:S(2)}) %collective-permute-start.4) | collective-permute-done | bytes 36896 | tf_op jit(solution)/shard_map/ppermute | solution.py:645
  93.6 0.6 collective-permute-done.3
  94.2 4.0 %all-to-all-done.2.refs_5_ = bf16[32,72,256]{2,1,0:T(8,128)(2,1)S(1)} async-done(((bf16[32,72,256]{2,1,0:T(8,128)(2,1)}), bf16[32,72,256]{2,1,0:T(8,128)(2,1)S(1)}, u32[]{:S(2)}, u32[]{:S(2)}) %all-to-all-start.2) | async-done | bytes 1179680 | tf_op jit(solution)/shard_map/all_to_all | solution.py:624
  98.2 1.0 copy-done
  99.2 0.0 copy-start.3
  99.3 0.0 copy-start.4
  99.3 0.0 copy-start.5
  99.3 13.8 %all_to_all.20.refs_1_ = bf16[16,72,256]{2,1,0:T(8,128)(2,1)S(1)} all-to-all(bf16[16,72,256]{2,1,0:T(8,128)(2,1)S(1)} %broadcast_in_dim.13), channel_id=1, replica_groups={{0,64,128,192,16,80,144,208,32,96,160,224,48,112,176,240},{4,68,132,196..., dimensions={0} | all-to-all | bytes 1179648 | tf_op jit(solution)/shard_map/all_to_all | solution.py:631
  113.1 2.6 %collective-permute-start.7 = (bf16[16,72,256]{2,1,0:T(8,128)(2,1)S(1)}, bf16[16,72,256]{2,1,0:T(8,128)(2,1)}, u32[]{:S(2)}, u32[]{:S(2)}) collective-permute-start(bf16[16,72,256]{2,1,0:T(8,128)(2,1)S(1)} %all_to_all.20.refs_1_), channel_id=1, source_target_pairs={{0,4},{4,0},{8,12},{12,8},{16,20},{20,16},{24,28},{28,24},{32,36},... | collective-permute-start | bytes 1769480 | tf_op jit(solution)/shard_map/ppermute | solution.py:651
  115.7 2.0 %shard_map.175 = bf16[32,32,256]{2,1,0:T(8,128)(2,1)} custom-call(bf16[32,32,256]{2,1,0:T(8,128)(2,1)} %bitcast.23, bf16[128,256]{1,0:T(8,128)(2,1)} %get-tuple-element.27.refs_1_), custom_call_target="tpu_custom_call" | custom-call | tf_op jit(solution)/shard_map/pallas_call | solution.py:74
  117.7 0.0 copy-done.3
  117.7 0.0 copy-done.4
  117.7 0.0 copy-done.5
  117.7 0.0 copy-start.1
  117.7 1.3 %copy-done.1 = bf16[32,72,256]{2,1,0:T(8,128)(2,1)S(1)} copy-done((bf16[32,72,256]{2,1,0:T(8,128)(2,1)S(1)}, bf16[32,72,256]{2,1,0:T(8,128)(2,1)}, u32[]{:S(2)}) %copy-start.1) | copy-done | bytes 1179672
  119.0 1.2 copy-done.2
  120.2 1.8 %shard_map.178 = bf16[32,32,256]{2,1,0:T(8,128)(2,1)} custom-call(s32[1]{0:T(128)} %bitcast.8.refs_0_, s32[4,64]{1,0:T(4,128)S(1)} %bitcast.17, s32[4,64]{1,0:T(4,128)S(1)} %bitcast.19, f32[32,32,256]{2,1,0:T(8,128)S(1)} %copy-done.2, f32[8,32,256]{2,1,0:T(8,128)S(1)} %copy-done.3, bf16[32,72,256]{2,1,0:T(8,128)(2,1)S(1)} %copy-done.1), custom_call_target="tpu_custom_call" | custom-call | tf_op jit(solution)/shard_map/pallas_call | solution.py:74
  122.0 0.0 collective-permute-done.7.refs_2_
  122.0 3.9 %shard_map.179 = (f32[9,256]{1,0:T(8,128)}, f32[4,256]{1,0:T(4,128)}, f32[256,1024]{1,0:T(8,128)}, f32[1,1024]{1,0:T(1,128)}, f32[1024,256]{1,0:T(8,128)}) custom-call(s32[1]{0:T(128)} %bitcast.8.refs_0_, bf16[16,72,256]{2,1,0:T(8,128)(2,1)S(1)} %all_to_all.20.refs_1_, bf16[16,72,256]{2,1,0:T(8,128)(2,1)} %collective-permute-done.7.refs_2_), custom_call_target="tpu_custom_call" | custom-call | tf_op jit(solution)/shard_map/pallas_call | solution.py:74
  (5 shorter events, 0.1 us)
Async XLA Ops:
  2.5 9.8 %collective-permute-start = (bf16[136,256]{1,0:T(8,128)(2,1)}, bf16[136,256]{1,0:T(8,128)(2,1)S(1)}, u32[]{:S(2)}, u32[]{:S(2)}) collective-permute-start(bf16[136,256]{1,0:T(8,128)(2,1)} %shard_map.172.refs_2_), channel_id=1, source_target_pairs={{0,8},{4,12},{8,0},{12,4},{16,24},{20,28},{24,16},{28,20},{32,40},... | collective-permute-start | bytes 208904 | tf_op jit(solution)/shard_map/ppermute | solution.py:677
  12.3 0.6 copy-start.6
  15.3 27.6 %all-to-all-start = ((bf16[32,72,256]{2,1,0:T(8,128)(2,1)}), bf16[32,72,256]{2,1,0:T(8,128)(2,1)}, u32[]{:S(2)}, u32[]{:S(2)}) async-start(bf16[32,72,256]{2,1,0:T(8,128)(2,1)} %shard_map.173), calls=%async_computation | async-start | bytes 2359296 | tf_op jit(solution)/shard_map/all_to_all | solution.py:624
  49.4 2.3 %collective-permute-start.1 = (bf16[16,72,256]{2,1,0:T(8,128)(2,1)}, bf16[16,72,256]{2,1,0:T(8,128)(2,1)S(1)}, u32[]{:S(2)}, u32[]{:S(2)}) collective-permute-start(bf16[16,72,256]{2,1,0:T(8,128)(2,1)} %get-tuple-element.32), channel_id=1, source_target_pairs={{0,4},{4,0},{8,12},{12,8},{16,20},{20,16},{24,28},{28,24},{32,36},... | collective-permute-start | bytes 1769480 | tf_op jit(solution)/shard_map/ppermute | solution.py:635
  53.9 16.8 %all-to-all-start.1 = ((bf16[16,72,256]{2,1,0:T(8,128)(2,1)}), bf16[16,72,256]{2,1,0:T(8,128)(2,1)S(1)}, u32[]{:S(2)}, u32[]{:S(2)}) async-start(bf16[16,72,256]{2,1,0:T(8,128)(2,1)} %add_convert_fusion), calls=%async_computation.1 | async-start | bytes 1179648 | tf_op jit(solution)/shard_map/all_to_all | solution.py:631
  59.3 8.5 %collective-permute-start.6 = (bf16[136,256]{1,0:T(8,128)(2,1)}, bf16[136,256]{1,0:T(8,128)(2,1)S(1)}, u32[]{:S(2)}, u32[]{:S(2)}) collective-permute-start(bf16[136,256]{1,0:T(8,128)(2,1)} %get-tuple-element.33.refs_2_), channel_id=1, source_target_pairs={{0,8},{4,12},{8,0},{12,4},{16,24},{20,28},{24,16},{28,20},{32,40},... | collective-permute-start | bytes 208904 | tf_op jit(solution)/shard_map/ppermute | solution.py:677
  67.7 0.6 copy-start.7
  70.8 27.4 %all-to-all-start.2 = ((bf16[32,72,256]{2,1,0:T(8,128)(2,1)}), bf16[32,72,256]{2,1,0:T(8,128)(2,1)S(1)}, u32[]{:S(2)}, u32[]{:S(2)}) async-start(bf16[32,72,256]{2,1,0:T(8,128)(2,1)} %shard_map.177), calls=%async_computation.2 | async-start | bytes 2359296 | tf_op jit(solution)/shard_map/all_to_all | solution.py:624
  79.7 7.5 %collective-permute-start.2 = (bf16[72,256]{1,0:T(8,128)(2,1)S(1)}, bf16[72,256]{1,0:T(8,128)(2,1)S(1)}, u32[]{:S(2)}, u32[]{:S(2)}) collective-permute-start(bf16[72,256]{1,0:T(8,128)(2,1)S(1)} %convert_reduce_fusion), channel_id=1, source_target_pairs={{0,8},{4,12},{8,0},{12,4},{16,24},{20,28},{24,16},{28,20},{32,40},... | collective-permute-start | bytes 110600 | tf_op jit(solution)/shard_map/ppermute | solution.py:641
  87.3 4.6 %collective-permute-start.5 = (bf16[72,256]{1,0:T(8,128)(2,1)S(1)}, bf16[72,256]{1,0:T(8,128)(2,1)S(1)}, u32[]{:S(2)}, u32[]{:S(2)}) collective-permute-start(bf16[72,256]{1,0:T(8,128)(2,1)S(1)} %add_convert_fusion.2), channel_id=1, source_target_pairs={{0,3},{1,0},{2,1},{3,2},{4,7},{5,4},{6,5},{7,6},{8,11},{9,8},{10,9... | collective-permute-start | bytes 110600 | tf_op jit(solution)/shard_map/ppermute | solution.py:645
  88.2 5.4 %collective-permute-start.4 = (bf16[72,256]{1,0:T(8,128)(2,1)S(1)}, bf16[72,256]{1,0:T(8,128)(2,1)S(1)}, u32[]{:S(2)}, u32[]{:S(2)}) collective-permute-start(bf16[72,256]{1,0:T(8,128)(2,1)S(1)} %add_convert_fusion.2), channel_id=1, source_target_pairs={{0,1},{1,2},{2,3},{3,0},{4,5},{5,6},{6,7},{7,4},{8,9},{9,10},{10,1... | collective-permute-start | bytes 110600 | tf_op jit(solution)/shard_map/ppermute | solution.py:645
  89.7 4.5 %collective-permute-start.3 = (bf16[72,256]{1,0:T(8,128)(2,1)S(1)}, bf16[72,256]{1,0:T(8,128)(2,1)S(1)}, u32[]{:S(2)}, u32[]{:S(2)}) collective-permute-start(bf16[72,256]{1,0:T(8,128)(2,1)S(1)} %add_convert_fusion.2), channel_id=1, source_target_pairs={{0,2},{1,3},{2,0},{3,1},{4,6},{5,7},{6,4},{7,5},{8,10},{9,11},{10,... | collective-permute-start | bytes 110600 | tf_op jit(solution)/shard_map/ppermute | solution.py:645
  98.2 1.0 copy-start
  99.2 18.5 %copy-start.3 = (f32[8,32,256]{2,1,0:T(8,128)S(1)}, f32[8,32,256]{2,1,0:T(8,128)}, u32[]{:S(2)}) copy-start(f32[8,32,256]{2,1,0:T(8,128)} %get-tuple-element.30.refs_4_) | copy-start | bytes 786436
  99.3 18.5 %copy-start.4 = (s32[64,4]{0,1:T(4,128)S(1)}, s32[64,4]{0,1:T(4,128)}, u32[]{:S(2)}) copy-start(s32[64,4]{0,1:T(4,128)} %param.22) | copy-start | bytes 3076
  99.3 18.5 %copy-start.5 = (s32[64,4]{0,1:T(4,128)S(1)}, s32[64,4]{0,1:T(4,128)}, u32[]{:S(2)}) copy-start(s32[64,4]{0,1:T(4,128)} %param.23) | copy-start | bytes 3076
  113.1 9.0 %collective-permute-start.7 = (bf16[16,72,256]{2,1,0:T(8,128)(2,1)S(1)}, bf16[16,72,256]{2,1,0:T(8,128)(2,1)}, u32[]{:S(2)}, u32[]{:S(2)}) collective-permute-start(bf16[16,72,256]{2,1,0:T(8,128)(2,1)S(1)} %all_to_all.20.refs_1_), channel_id=1, source_target_pairs={{0,4},{4,0},{8,12},{12,8},{16,20},{20,16},{24,28},{28,24},{32,36},... | collective-permute-start | bytes 1769480 | tf_op jit(solution)/shard_map/ppermute | solution.py:651
  117.7 1.3 %copy-start.1 = (bf16[32,72,256]{2,1,0:T(8,128)(2,1)S(1)}, bf16[32,72,256]{2,1,0:T(8,128)(2,1)}, u32[]{:S(2)}) copy-start(bf16[32,72,256]{2,1,0:T(8,128)(2,1)} %copy-done) | copy-start | bytes 3538948
  119.0 1.2 copy-start.2

commit v3 on v2

--- a/solution.py
+++ b/solution.py
@@ -336,6 +336,46 @@
     lax.fori_loop(0, 8, inner_rows, 0)
 
 
+def put_rim(d_lines, kern_ref, lines_ref, rim_ref):
+    last = S - 1
+    spot = lambda line, i: line[i : i + 1]
+    place = lax.broadcasted_iota(jnp.int32, (S, C), 0)
+    flat = lambda k: kern_ref[k : k + 1, :]
+
+    def spread(line, taps):
+        back = jnp.where(place == last, 0.0, pltpu.roll(line, last, 0))
+        ahead = jnp.where(place == 0, 0.0, pltpu.roll(line, 1, 0))
+        return back * flat(taps[0]) + line * flat(taps[1]) + ahead * flat(taps[2])
+
+    def whole(line, at):
+        line = jnp.where(place == 0, spot(d_lines[0], at), line)
+        return jnp.where(place == last, spot(d_lines[1], at), line)
+
+    row_taps = lambda u: (3 * u, 3 * u + 1, 3 * u + 2)
+    col_taps = lambda v: (v, 3 + v, 6 + v)
+    rim = [
+        spread(d_lines[0], row_taps(0)),
+        spread(d_lines[1], row_taps(2)),
+        spread(whole(d_lines[2], 0), col_taps(0)),
+        spread(whole(d_lines[3], last), col_taps(2)),
+    ]
+    corners = [
+        spot(d_lines[0], 0) * flat(0),
+        spot(d_lines[0], last) * flat(2),
+        spot(d_lines[1], 0) * flat(6),
+        spot(d_lines[1], last) * flat(8),
+    ]
+    put_edges(rim_ref, rim, corners)
+    lines_ref[0] = spread(d_lines[0], row_taps(1))
+    lines_ref[1] = spread(d_lines[0], row_taps(2))
+    lines_ref[2] = spread(d_lines[1], row_taps(0))
+    lines_ref[3] = spread(d_lines[1], row_taps(1))
+    lines_ref[4] = spread(d_lines[2], col_taps(1))
+    lines_ref[5] = spread(d_lines[2], col_taps(2))
+    lines_ref[6] = spread(d_lines[3], col_taps(0))
+    lines_ref[7] = spread(d_lines[3], col_taps(1))
+
+
 def border_kernel(
     waits,
     pos_ref,
@@ -353,7 +393,8 @@
     w_out_ref,
     grad_ref,
     rows_ref,
-    dconv_ref,
+    lines_ref,
+    rim_ref,
     own_ref,
     send_ref,
 ):
@@ -439,7 +480,7 @@
     *g_bin, g_gain, g_shift = sums
     d_lines = [dconv[S * n : S * n + S] for n in range(4)]
 
-    dconv_ref[...] = dconv
+    put_rim(d_lines, kern_ref, lines_ref, rim_ref)
 
     waits[13]()
 
@@ -479,47 +520,6 @@
         @pl.when(core != j // 16)
         def _(row=row, j=j):
             send_ref[j % 16, pl.ds(64, CHUNK - 64), :] = row.astype(BF)
-
-
-def rim_kernel(waits, dconv_ref, kern_ref, lines_ref, rim_ref):
-    last = S - 1
-    spot = lambda line, i: line[i : i + 1]
-    place = lax.broadcasted_iota(jnp.int32, (S, C), 0)
-    flat = lambda k: kern_ref[k : k + 1, :]
-    d_lines = [dconv_ref[S * n : S * n + S] for n in range(4)]
-
-    def spread(line, taps):
-        back = jnp.where(place == last, 0.0, pltpu.roll(line, last, 0))
-        ahead = jnp.where(place == 0, 0.0, pltpu.roll(line, 1, 0))
-        return back * flat(taps[0]) + line * flat(taps[1]) + ahead * flat(taps[2])
-
-    def whole(line, at):
-        line = jnp.where(place == 0, spot(d_lines[0], at), line)
-        return jnp.where(place == last, spot(d_lines[1], at), line)
-
-    row_taps = lambda u: (3 * u, 3 * u + 1, 3 * u + 2)
-    col_taps = lambda v: (v, 3 + v, 6 + v)
-    rim = [
-        spread(d_lines[0], row_taps(0)),
-        spread(d_lines[1], row_taps(2)),
-        spread(whole(d_lines[2], 0), col_taps(0)),
-        spread(whole(d_lines[3], last), col_taps(2)),
-    ]
-    corners = [
-        spot(d_lines[0], 0) * flat(0),
-        spot(d_lines[0], last) * flat(2),
-        spot(d_lines[1], 0) * flat(6),
-        spot(d_lines[1], last) * flat(8),
-    ]
-    put_edges(rim_ref, rim, corners)
-    lines_ref[0] = spread(d_lines[0], row_taps(1))
-    lines_ref[1] = spread(d_lines[0], row_taps(2))
-    lines_ref[2] = spread(d_lines[1], row_taps(0))
-    lines_ref[3] = spread(d_lines[1], row_taps(1))
-    lines_ref[4] = spread(d_lines[2], col_taps(1))
-    lines_ref[5] = spread(d_lines[2], col_taps(2))
-    lines_ref[6] = spread(d_lines[3], col_taps(0))
-    lines_ref[7] = spread(d_lines[3], col_taps(1))
 
 
 def patch_kernel(waits, part_ref, rows_ref, blocks_ref, wide_ref):
@@ -723,7 +723,7 @@
         ),
     )
     where = [(here, "smem", 0), (links, "smem", 0), (diagonals, "smem", 0)]
-    border_rows, dconv, own, send = staged_call(
+    border_rows, lines, rim, own, send = staged_call(
         border_kernel,
         where
         + [(border_lines, "vmem", 0), (halo, "vmem", 0)]
@@ -731,17 +731,11 @@
         + [(grads, "vmem", 1)],
         [
             (sds((4 * S, C), BF), True),
-            (sds((4 * S, C), F32), True),
+            (sds((8, S, C), F32), True),
+            (edges, True),
             (sds((16, CHUNK, C), F32), True),
             (sds((16, CHUNK, C), BF), True),
         ],
-        [],
-        63,
-    )
-    lines, rim = staged_call(
-        rim_kernel,
-        [(dconv, "vmem", 0), (dw_kernel, "vmem", 0)],
-        [(sds((8, S, C), F32), True), (edges, True)],
         [],
         63,
     )

time: 127 us -> 125 us (0.984)
  Pallas kernels: 37.5 us -> 36 us
    pallas_call x9 -> x8, Pallas kernels: 37.5 us -> 36 us  [staged_call(): pl.pallas_call(body, out_shape=tuple((o for o, _ in outs)), in_specs=[VME...]
    unnamed x16 -> x18, local copies, waits for them, and re-layouts: 4.79 us -> 4.8 us
  transfers between devices with their start and end apart: 11 -> 11, of which waited for: 8 -> 8; matrix products, arithmetic and copies ran while one was open for 0% -> 0% of each run, Pallas kernels for 18% -> 17%
where the time goes in v3:
time: 125 us; the launch traced here: 124 us
  starting transfers between devices  49.1 us (39%)
  Pallas kernels  36 us (29%)
  waiting for transfers between devices  17.5 us (14%)
  blocking collectives  13.7 us (11%)
  local copies, waits for them, and re-layouts  4.84 us (4%)
  other arithmetic  2.33 us (2%)
    pallas_call x8, Pallas kernels, staged_call(): pl.pallas_call(body, out_shape=tuple((o for o, _ in outs)), in_specs=[VME...  36 us
    all_to_all x2, starting transfers between devices, exchange(): lax.all_to_all(slots, 'space', 0, 0, axis_index_groups=halves, tiled=True)  17.8 us
    ppermute x2, starting transfers between devices, to_slots(): other = lax.ppermute(mine, 'space', moves('h', 1))  13.9 us
    all_to_all x1, blocking collectives, plane(): lax.all_to_all(slots, 'space', 0, 0, axis_index_groups=planes, tiled=True)  13.7 us
    all_to_all x2, waiting for transfers between devices, exchange(): lax.all_to_all(slots, 'space', 0, 0, axis_index_groups=halves, tiled=True)  7.49 us
    ppermute x1, starting transfers between devices, sum_over_devices(): other = lax.ppermute(mine, 'space', moves('h', 1))  6.16 us
    unnamed x18, local copies, waits for them, and re-layouts  4.8 us
    ppermute x3, starting transfers between devices, sum_over_devices(): got = [mine] + [lax.ppermute(mine, 'batch', turn(d)) for d in (1, 2, 3)]  4.38 us
  transfers between devices with their start and end apart: 11, of which 8 were waited for; matrix products, arithmetic and copies ran while one was open for 0% of the time, Pallas kernels for 17%

profile of v3, /device:TPU:1, one launch (start us, length us, event | category | flops | bytes accessed | tf_op | source)
XLA Modules:
  0.0 124.4 jit_solution(16133012303284915770)
XLA Ops:
  0.6 1.8 %shard_map.172.refs_2_ = bf16[136,256]{1,0:T(8,128)(2,1)} custom-call(bf16[32,32,256]{2,1,0:T(8,128)(2,1)} %bitcast.21), custom_call_target="tpu_custom_call" | custom-call | tf_op jit(solution)/shard_map/pallas_call | solution.py:74
  2.5 7.8 %collective-permute-start = (bf16[136,256]{1,0:T(8,128)(2,1)}, bf16[136,256]{1,0:T(8,128)(2,1)S(1)}, u32[]{:S(2)}, u32[]{:S(2)}) collective-permute-start(bf16[136,256]{1,0:T(8,128)(2,1)} %shard_map.172.refs_2_), channel_id=1, source_target_pairs={{0,8},{4,12},{8,0},{12,4},{16,24},{20,28},{24,16},{28,20},{32,40},... | collective-permute-start | bytes 208904 | tf_op jit(solution)/shard_map/ppermute | solution.py:677
  10.3 2.0 %collective-permute-done.refs_3_ = bf16[136,256]{1,0:T(8,128)(2,1)S(1)} collective-permute-done((bf16[136,256]{1,0:T(8,128)(2,1)}, bf16[136,256]{1,0:T(8,128)(2,1)S(1)}, u32[]{:S(2)}, u32[]{:S(2)}) %collective-permute-start) | collective-permute-done | bytes 69664 | tf_op jit(solution)/shard_map/ppermute | solution.py:677
  12.3 0.0 copy-start.7
  12.3 0.6 copy-done.7
  12.9 2.4 %shard_map.173 = bf16[32,72,256]{2,1,0:T(8,128)(2,1)} custom-call(s32[1]{0:T(128)} %bitcast.8.refs_0_, s32[4,64]{1,0:T(4,128)} %bitcast.14, bf16[136,256]{1,0:T(8,128)(2,1)} %shard_map.172.refs_2_, bf16[136,256]{1,0:T(8,128)(2,1)} %copy-done.7), custom_call_target="tpu_custom_call" | custom-call | tf_op jit(solution)/shard_map/pallas_call | solution.py:74
  15.3 9.0 %all-to-all-start = ((bf16[32,72,256]{2,1,0:T(8,128)(2,1)}), bf16[32,72,256]{2,1,0:T(8,128)(2,1)}, u32[]{:S(2)}, u32[]{:S(2)}) async-start(bf16[32,72,256]{2,1,0:T(8,128)(2,1)} %shard_map.173), calls=%async_computation | async-start | bytes 2359296 | tf_op jit(solution)/shard_map/all_to_all | solution.py:624
  24.3 15.0 %shard_map.171 = (bf16[1024,256]{1,0:T(8,128)(2,1)}, f32[32,32,256]{2,1,0:T(8,128)}, f32[32,72,256]{2,1,0:T(8,128)}, bf16[12,32,256]{2,1,0:T(8,128)(2,1)}) custom-call(bf16[32,32,256]{2,1,0:T(8,128)(2,1)} %bitcast.22, bf16[1024,256]{1,0:T(8,128)(2,1)} %bitcast.35, f32[9,256]{1,0:T(8,128)} %refs_5_.1, f32[1,256]{1,0:T(1,128)} %bitcast.27, f32[1,256]{1,0:T(1,128)} %bitcast.29, ...), custom_call_target="tpu_custom_call" | custom-call | flops 3221225472 | bytes 8388608 | tf_op jit(solution)/shard_map/pallas_call | solution.py:74
  39.3 3.6 %all-to-all-done.refs_4_ = bf16[32,72,256]{2,1,0:T(8,128)(2,1)} async-done(((bf16[32,72,256]{2,1,0:T(8,128)(2,1)}), bf16[32,72,256]{2,1,0:T(8,128)(2,1)}, u32[]{:S(2)}, u32[]{:S(2)}) %all-to-all-start) | async-done | bytes 1179680 | tf_op jit(solution)/shard_map/all_to_all | solution.py:624
  42.9 6.6 %shard_map.174 = (bf16[128,256]{1,0:T(8,128)(2,1)}, f32[8,32,256]{2,1,0:T(8,128)}, bf16[136,256]{1,0:T(8,128)(2,1)}, f32[16,72,256]{2,1,0:T(8,128)}, bf16[16,72,256]{2,1,0:T(8,128)(2,1)}) custom-call(s32[1]{0:T(128)} %bitcast.8.refs_0_, s32[4,64]{1,0:T(4,128)} %bitcast.15, s32[4,64]{1,0:T(4,128)} %bitcast.18, ...), custom_call_target="tpu_custom_call" | custom-call | tf_op jit(solution)/shard_map/pallas_call | solution.py:74
  49.6 0.5 collective-permute-start.1
  50.1 1.8 %collective-permute-done.1 = bf16[16,72,256]{2,1,0:T(8,128)(2,1)S(1)} collective-permute-done((bf16[16,72,256]{2,1,0:T(8,128)(2,1)}, bf16[16,72,256]{2,1,0:T(8,128)(2,1)S(1)}, u32[]{:S(2)}, u32[]{:S(2)}) %collective-permute-start.1) | collective-permute-done | bytes 589856 | tf_op jit(solution)/shard_map/ppermute | solution.py:635
  51.9 2.2 %add_convert_fusion = bf16[16,72,256]{2,1,0:T(8,128)(2,1)} fusion(f32[16,72,256]{2,1,0:T(8,128)} %get-tuple-element.29, bf16[16,72,256]{2,1,0:T(8,128)(2,1)S(1)} %collective-permute-done.1), kind=kLoop, calls=%fused_computation.1 | loop fusion | flops 884736 | bytes 2359296 | tf_op jit(solution)/shard_map/convert_element_type | solution.py:636
  54.1 0.0 copy-start.6
  54.1 3.7 %all-to-all-start.1 = ((bf16[16,72,256]{2,1,0:T(8,128)(2,1)}), bf16[16,72,256]{2,1,0:T(8,128)(2,1)S(1)}, u32[]{:S(2)}, u32[]{:S(2)}) async-start(bf16[16,72,256]{2,1,0:T(8,128)(2,1)} %add_convert_fusion), calls=%async_computation.1 | async-start | bytes 1179648 | tf_op jit(solution)/shard_map/all_to_all | solution.py:631
  57.8 0.0 copy-done.6
  57.9 6.1 %collective-permute-start.6 = (bf16[136,256]{1,0:T(8,128)(2,1)S(1)}, bf16[136,256]{1,0:T(8,128)(2,1)S(1)}, u32[]{:S(2)}, u32[]{:S(2)}) collective-permute-start(bf16[136,256]{1,0:T(8,128)(2,1)S(1)} %copy-done.6), channel_id=1, source_target_pairs={{0,8},{4,12},{8,0},{12,4},{16,24},{20,28},{24,16},{28,20},{32,40},... | collective-permute-start | bytes 208904 | tf_op jit(solution)/shard_map/ppermute | solution.py:677
  63.9 2.2 %collective-permute-done.6.refs_3_ = bf16[136,256]{1,0:T(8,128)(2,1)S(1)} collective-permute-done((bf16[136,256]{1,0:T(8,128)(2,1)S(1)}, bf16[136,256]{1,0:T(8,128)(2,1)S(1)}, u32[]{:S(2)}, u32[]{:S(2)}) %collective-permute-start.6) | collective-permute-done | bytes 69664 | tf_op jit(solution)/shard_map/ppermute | solution.py:677
  66.1 0.6 copy-done.8
  66.7 2.4 %shard_map.176 = bf16[32,72,256]{2,1,0:T(8,128)(2,1)} custom-call(s32[1]{0:T(128)} %bitcast.8.refs_0_, s32[4,64]{1,0:T(4,128)} %bitcast.16, bf16[136,256]{1,0:T(8,128)(2,1)} %get-tuple-element.31.refs_2_, bf16[136,256]{1,0:T(8,128)(2,1)} %copy-done.8), custom_call_target="tpu_custom_call" | custom-call | tf_op jit(solution)/shard_map/pallas_call | solution.py:74
  69.1 0.0 all-to-all-done.1
  69.1 8.8 %all-to-all-start.2 = ((bf16[32,72,256]{2,1,0:T(8,128)(2,1)}), bf16[32,72,256]{2,1,0:T(8,128)(2,1)S(1)}, u32[]{:S(2)}, u32[]{:S(2)}) async-start(bf16[32,72,256]{2,1,0:T(8,128)(2,1)} %shard_map.176), calls=%async_computation.2 | async-start | bytes 2359296 | tf_op jit(solution)/shard_map/all_to_all | solution.py:624
  77.9 0.1 convert_reduce_fusion
  78.0 6.2 %collective-permute-start.2 = (bf16[72,256]{1,0:T(8,128)(2,1)S(1)}, bf16[72,256]{1,0:T(8,128)(2,1)S(1)}, u32[]{:S(2)}, u32[]{:S(2)}) collective-permute-start(bf16[72,256]{1,0:T(8,128)(2,1)S(1)} %convert_reduce_fusion), channel_id=1, source_target_pairs={{0,8},{4,12},{8,0},{12,4},{16,24},{20,28},{24,16},{28,20},{32,40},... | collective-permute-start | bytes 110600 | tf_op jit(solution)/shard_map/ppermute | solution.py:641
  84.2 1.6 %collective-permute-done.2 = bf16[72,256]{1,0:T(8,128)(2,1)S(1)} collective-permute-done((bf16[72,256]{1,0:T(8,128)(2,1)S(1)}, bf16[72,256]{1,0:T(8,128)(2,1)S(1)}, u32[]{:S(2)}, u32[]{:S(2)}) %collective-permute-start.2) | collective-permute-done | bytes 36896 | tf_op jit(solution)/shard_map/ppermute | solution.py:641
  85.8 0.7 collective-permute-start.5
  86.6 1.5 %collective-permute-start.4 = (bf16[72,256]{1,0:T(8,128)(2,1)S(1)}, bf16[72,256]{1,0:T(8,128)(2,1)S(1)}, u32[]{:S(2)}, u32[]{:S(2)}) collective-permute-start(bf16[72,256]{1,0:T(8,128)(2,1)S(1)} %add_convert_fusion.2), channel_id=1, source_target_pairs={{0,1},{1,2},{2,3},{3,0},{4,5},{5,6},{6,7},{7,4},{8,9},{9,10},{10,1... | collective-permute-start | bytes 110600 | tf_op jit(solution)/shard_map/ppermute | solution.py:645
  88.0 2.2 %collective-permute-start.3 = (bf16[72,256]{1,0:T(8,128)(2,1)S(1)}, bf16[72,256]{1,0:T(8,128)(2,1)S(1)}, u32[]{:S(2)}, u32[]{:S(2)}) collective-permute-start(bf16[72,256]{1,0:T(8,128)(2,1)S(1)} %add_convert_fusion.2), channel_id=1, source_target_pairs={{0,2},{1,3},{2,0},{3,1},{4,6},{5,7},{6,4},{7,5},{8,10},{9,11},{10,... | collective-permute-start | bytes 110600 | tf_op jit(solution)/shard_map/ppermute | solution.py:645
  90.2 0.0 collective-permute-done.5
  90.2 1.7 %collective-permute-done.4 = bf16[72,256]{1,0:T(8,128)(2,1)S(1)} collective-permute-done((bf16[72,256]{1,0:T(8,128)(2,1)S(1)}, bf16[72,256]{1,0:T(8,128)(2,1)S(1)}, u32[]{:S(2)}, u32[]{:S(2)}) %collective-permute-start.4) | collective-permute-done | bytes 36896 | tf_op jit(solution)/shard_map/ppermute | solution.py:645
  91.9 0.6 collective-permute-done.3
  92.5 3.9 %all-to-all-done.2.refs_5_ = bf16[32,72,256]{2,1,0:T(8,128)(2,1)S(1)} async-done(((bf16[32,72,256]{2,1,0:T(8,128)(2,1)}), bf16[32,72,256]{2,1,0:T(8,128)(2,1)S(1)}, u32[]{:S(2)}, u32[]{:S(2)}) %all-to-all-start.2) | async-done | bytes 1179680 | tf_op jit(solution)/shard_map/all_to_all | solution.py:624
  96.4 1.0 copy-done
  97.5 0.0 copy-start.3
  97.5 0.0 copy-start.4
  97.5 0.0 copy-start.5
  97.6 13.7 %all_to_all.20.refs_1_ = bf16[16,72,256]{2,1,0:T(8,128)(2,1)S(1)} all-to-all(bf16[16,72,256]{2,1,0:T(8,128)(2,1)S(1)} %broadcast_in_dim.13), channel_id=1, replica_groups={{0,64,128,192,16,80,144,208,32,96,160,224,48,112,176,240},{4,68,132,196..., dimensions={0} | all-to-all | bytes 1179648 | tf_op jit(solution)/shard_map/all_to_all | solution.py:631
  111.3 2.7 %collective-permute-start.7 = (bf16[16,72,256]{2,1,0:T(8,128)(2,1)S(1)}, bf16[16,72,256]{2,1,0:T(8,128)(2,1)}, u32[]{:S(2)}, u32[]{:S(2)}) collective-permute-start(bf16[16,72,256]{2,1,0:T(8,128)(2,1)S(1)} %all_to_all.20.refs_1_), channel_id=1, source_target_pairs={{0,4},{4,0},{8,12},{12,8},{16,20},{20,16},{24,28},{28,24},{32,36},... | collective-permute-start | bytes 1769480 | tf_op jit(solution)/shard_map/ppermute | solution.py:651
  113.9 2.0 %shard_map.175 = bf16[32,32,256]{2,1,0:T(8,128)(2,1)} custom-call(bf16[32,32,256]{2,1,0:T(8,128)(2,1)} %bitcast.23, bf16[128,256]{1,0:T(8,128)(2,1)} %get-tuple-element.26.refs_1_), custom_call_target="tpu_custom_call" | custom-call | tf_op jit(solution)/shard_map/pallas_call | solution.py:74
  116.0 0.0 copy-done.3
  116.0 0.0 copy-done.4
  116.0 0.0 copy-done.5
  116.0 0.0 copy-start.1
  116.0 1.3 %copy-done.1 = bf16[32,72,256]{2,1,0:T(8,128)(2,1)S(1)} copy-done((bf16[32,72,256]{2,1,0:T(8,128)(2,1)S(1)}, bf16[32,72,256]{2,1,0:T(8,128)(2,1)}, u32[]{:S(2)}) %copy-start.1) | copy-done | bytes 1179672
  117.3 1.2 copy-done.2
  118.5 1.8 %shard_map.177 = bf16[32,32,256]{2,1,0:T(8,128)(2,1)} custom-call(s32[1]{0:T(128)} %bitcast.8.refs_0_, s32[4,64]{1,0:T(4,128)S(1)} %bitcast.17, s32[4,64]{1,0:T(4,128)S(1)} %bitcast.19, f32[32,32,256]{2,1,0:T(8,128)S(1)} %copy-done.2, f32[8,32,256]{2,1,0:T(8,128)S(1)} %copy-done.3, bf16[32,72,256]{2,1,0:T(8,128)(2,1)S(1)} %copy-done.1), custom_call_target="tpu_custom_call" | custom-call | tf_op jit(solution)/shard_map/pallas_call | solution.py:74
  120.3 0.0 collective-permute-done.7.refs_2_
  120.3 3.9 %shard_map.178 = (f32[9,256]{1,0:T(8,128)}, f32[4,256]{1,0:T(4,128)}, f32[256,1024]{1,0:T(8,128)}, f32[1,1024]{1,0:T(1,128)}, f32[1024,256]{1,0:T(8,128)}) custom-call(s32[1]{0:T(128)} %bitcast.8.refs_0_, bf16[16,72,256]{2,1,0:T(8,128)(2,1)S(1)} %all_to_all.20.refs_1_, bf16[16,72,256]{2,1,0:T(8,128)(2,1)} %collective-permute-done.7.refs_2_), custom_call_target="tpu_custom_call" | custom-call | tf_op jit(solution)/shard_map/pallas_call | solution.py:74
  (6 shorter events, 0.1 us)
Async XLA Ops:
  2.5 9.8 %collective-permute-start = (bf16[136,256]{1,0:T(8,128)(2,1)}, bf16[136,256]{1,0:T(8,128)(2,1)S(1)}, u32[]{:S(2)}, u32[]{:S(2)}) collective-permute-start(bf16[136,256]{1,0:T(8,128)(2,1)} %shard_map.172.refs_2_), channel_id=1, source_target_pairs={{0,8},{4,12},{8,0},{12,4},{16,24},{20,28},{24,16},{28,20},{32,40},... | collective-permute-start | bytes 208904 | tf_op jit(solution)/shard_map/ppermute | solution.py:677
  12.3 0.6 copy-start.7
  15.3 27.6 %all-to-all-start = ((bf16[32,72,256]{2,1,0:T(8,128)(2,1)}), bf16[32,72,256]{2,1,0:T(8,128)(2,1)}, u32[]{:S(2)}, u32[]{:S(2)}) async-start(bf16[32,72,256]{2,1,0:T(8,128)(2,1)} %shard_map.173), calls=%async_computation | async-start | bytes 2359296 | tf_op jit(solution)/shard_map/all_to_all | solution.py:624
  49.6 2.3 %collective-permute-start.1 = (bf16[16,72,256]{2,1,0:T(8,128)(2,1)}, bf16[16,72,256]{2,1,0:T(8,128)(2,1)S(1)}, u32[]{:S(2)}, u32[]{:S(2)}) collective-permute-start(bf16[16,72,256]{2,1,0:T(8,128)(2,1)} %get-tuple-element.30), channel_id=1, source_target_pairs={{0,4},{4,0},{8,12},{12,8},{16,20},{20,16},{24,28},{28,24},{32,36},... | collective-permute-start | bytes 1769480 | tf_op jit(solution)/shard_map/ppermute | solution.py:635
  54.1 3.7 %copy-start.6 = (bf16[136,256]{1,0:T(8,128)(2,1)S(1)}, bf16[136,256]{1,0:T(8,128)(2,1)}, u32[]{:S(2)}) copy-start(bf16[136,256]{1,0:T(8,128)(2,1)} %get-tuple-element.31.refs_2_) | copy-start | bytes 208900
  54.1 15.0 %all-to-all-start.1 = ((bf16[16,72,256]{2,1,0:T(8,128)(2,1)}), bf16[16,72,256]{2,1,0:T(8,128)(2,1)S(1)}, u32[]{:S(2)}, u32[]{:S(2)}) async-start(bf16[16,72,256]{2,1,0:T(8,128)(2,1)} %add_convert_fusion), calls=%async_computation.1 | async-start | bytes 1179648 | tf_op jit(solution)/shard_map/all_to_all | solution.py:631
  57.9 8.2 %collective-permute-start.6 = (bf16[136,256]{1,0:T(8,128)(2,1)S(1)}, bf16[136,256]{1,0:T(8,128)(2,1)S(1)}, u32[]{:S(2)}, u32[]{:S(2)}) collective-permute-start(bf16[136,256]{1,0:T(8,128)(2,1)S(1)} %copy-done.6), channel_id=1, source_target_pairs={{0,8},{4,12},{8,0},{12,4},{16,24},{20,28},{24,16},{28,20},{32,40},... | collective-permute-start | bytes 208904 | tf_op jit(solution)/shard_map/ppermute | solution.py:677
  66.1 0.6 copy-start.8
  69.1 27.3 %all-to-all-start.2 = ((bf16[32,72,256]{2,1,0:T(8,128)(2,1)}), bf16[32,72,256]{2,1,0:T(8,128)(2,1)S(1)}, u32[]{:S(2)}, u32[]{:S(2)}) async-start(bf16[32,72,256]{2,1,0:T(8,128)(2,1)} %shard_map.176), calls=%async_computation.2 | async-start | bytes 2359296 | tf_op jit(solution)/shard_map/all_to_all | solution.py:624
  78.0 7.8 %collective-permute-start.2 = (bf16[72,256]{1,0:T(8,128)(2,1)S(1)}, bf16[72,256]{1,0:T(8,128)(2,1)S(1)}, u32[]{:S(2)}, u32[]{:S(2)}) collective-permute-start(bf16[72,256]{1,0:T(8,128)(2,1)S(1)} %convert_reduce_fusion), channel_id=1, source_target_pairs={{0,8},{4,12},{8,0},{12,4},{16,24},{20,28},{24,16},{28,20},{32,40},... | collective-permute-start | bytes 110600 | tf_op jit(solution)/shard_map/ppermute | solution.py:641
  85.8 4.4 %collective-permute-start.5 = (bf16[72,256]{1,0:T(8,128)(2,1)S(1)}, bf16[72,256]{1,0:T(8,128)(2,1)S(1)}, u32[]{:S(2)}, u32[]{:S(2)}) collective-permute-start(bf16[72,256]{1,0:T(8,128)(2,1)S(1)} %add_convert_fusion.2), channel_id=1, source_target_pairs={{0,3},{1,0},{2,1},{3,2},{4,7},{5,4},{6,5},{7,6},{8,11},{9,8},{10,9... | collective-permute-start | bytes 110600 | tf_op jit(solution)/shard_map/ppermute | solution.py:645
  86.6 5.4 %collective-permute-start.4 = (bf16[72,256]{1,0:T(8,128)(2,1)S(1)}, bf16[72,256]{1,0:T(8,128)(2,1)S(1)}, u32[]{:S(2)}, u32[]{:S(2)}) collective-permute-start(bf16[72,256]{1,0:T(8,128)(2,1)S(1)} %add_convert_fusion.2), channel_id=1, source_target_pairs={{0,1},{1,2},{2,3},{3,0},{4,5},{5,6},{6,7},{7,4},{8,9},{9,10},{10,1... | collective-permute-start | bytes 110600 | tf_op jit(solution)/shard_map/ppermute | solution.py:645
  88.0 4.5 %collective-permute-start.3 = (bf16[72,256]{1,0:T(8,128)(2,1)S(1)}, bf16[72,256]{1,0:T(8,128)(2,1)S(1)}, u32[]{:S(2)}, u32[]{:S(2)}) collective-permute-start(bf16[72,256]{1,0:T(8,128)(2,1)S(1)} %add_convert_fusion.2), channel_id=1, source_target_pairs={{0,2},{1,3},{2,0},{3,1},{4,6},{5,7},{6,4},{7,5},{8,10},{9,11},{10,... | collective-permute-start | bytes 110600 | tf_op jit(solution)/shard_map/ppermute | solution.py:645
  96.4 1.0 copy-start
  97.5 18.5 %copy-start.3 = (f32[8,32,256]{2,1,0:T(8,128)S(1)}, f32[8,32,256]{2,1,0:T(8,128)}, u32[]{:S(2)}) copy-start(f32[8,32,256]{2,1,0:T(8,128)} %get-tuple-element.28.refs_4_) | copy-start | bytes 786436
  97.5 18.5 %copy-start.4 = (s32[64,4]{0,1:T(4,128)S(1)}, s32[64,4]{0,1:T(4,128)}, u32[]{:S(2)}) copy-start(s32[64,4]{0,1:T(4,128)} %param.22) | copy-start | bytes 3076
  97.5 18.5 %copy-start.5 = (s32[64,4]{0,1:T(4,128)S(1)}, s32[64,4]{0,1:T(4,128)}, u32[]{:S(2)}) copy-start(s32[64,4]{0,1:T(4,128)} %param.23) | copy-start | bytes 3076
  111.3 9.0 %collective-permute-start.7 = (bf16[16,72,256]{2,1,0:T(8,128)(2,1)S(1)}, bf16[16,72,256]{2,1,0:T(8,128)(2,1)}, u32[]{:S(2)}, u32[]{:S(2)}) collective-permute-start(bf16[16,72,256]{2,1,0:T(8,128)(2,1)S(1)} %all_to_all.20.refs_1_), channel_id=1, source_target_pairs={{0,4},{4,0},{8,12},{12,8},{16,20},{20,16},{24,28},{28,24},{32,36},... | collective-permute-start | bytes 1769480 | tf_op jit(solution)/shard_map/ppermute | solution.py:651
  116.0 1.3 %copy-start.1 = (bf16[32,72,256]{2,1,0:T(8,128)(2,1)S(1)}, bf16[32,72,256]{2,1,0:T(8,128)(2,1)}, u32[]{:S(2)}) copy-start(bf16[32,72,256]{2,1,0:T(8,128)(2,1)} %copy-done) | copy-start | bytes 3538948
  117.3 1.2 copy-start.2
